TPU v7x, 512 devices: a whole 4x8x8 slice. The times are simulated.
512 devices in a mesh: expert: 128 (over z, y, core), dp: 4 (over x).
Axes of the slice: x: 4, y: 8, z: 8, core: 2. Of those that a mesh axis runs over, the one named last changes fastest.
Arguments:
- inputs: bfloat16 [65536, 256], P(('expert', 'dp')), may hold values from -4 to 4
- out_grad: bfloat16 [65536, 2048], P(('expert', 'dp')), may hold values from -6 to 6
- route: int32 [65536, 1], P(('expert', 'dp')), may hold values from 0 to 31; in each aligned block of 128 rows (0 to 127, 128 to 255, ...) at most 8 rows name the same one
- coef: bfloat16 [128, 256, 8, 512], P('expert', 'dp'), may hold values from -0.125 to 0.125
- first_moment: bfloat16 [128, 256, 8, 512], P('expert', 'dp'), may hold values from -15 to 15
- second_moment: bfloat16 [128, 256, 8, 512], P('expert', 'dp'), may hold values from 1 to 100
Outputs:
- input_grad: bfloat16 [65536, 256], P(('expert', 'dp'))
- new_coef: bfloat16 [128, 256, 8, 512], P('expert', 'dp')
- new_first: bfloat16 [128, 256, 8, 512], P('expert', 'dp')
- new_second: bfloat16 [128, 256, 8, 512], P('expert', 'dp')
Inputs may be any that keep to these rules, and one draw needn't show every extreme that they name: `route`: each row names one expert. Among the rows of one device no expert is named by more than 8 rows, and on some device one expert is named by exactly 8 rows.
All inputs are finite; a program needn't handle non-finite values.
Results may differ from a plain program's by a relative error of at most 0.0085.
Values may be sent and summed in bfloat16 or wider, within the bound.
No kernel may reach another device: no remote copies, remote signals or barrier semaphores. Data moves between devices by JAX's collectives and lax.ppermute only.
A program may use at most 64 MiB of HBM per device.

v0:
```python
import jax
import jax.numpy as jnp
from jax import lax
from jax.sharding import PartitionSpec as P

IN = 256
NB = 8
SPLIT = 4
COLS = 512


GRID_LOWER = -2.0
GRID_UPPER = 2.0
PENALTY = 10.0
LEARN_RATE = 0.001
BETA_ONE = 0.9
BETA_TWO = 0.999
EPSILON = 1e-08
WEIGHT_DECAY = 0.1
BIAS_ONE = 0.999973438601112
BIAS_TWO = 0.0952078528855534


def spline_bases(values):
    spacing = (GRID_UPPER - GRID_LOWER) / (NB - 3)
    offset = (values - (GRID_LOWER - 3.0 * spacing)) / spacing
    shifted = offset[..., None] - jnp.arange(NB, dtype=jnp.float32)
    inside = shifted < 4.0
    part_zero = jnp.maximum(shifted, 0.0)
    part_one = jnp.maximum(shifted - 1.0, 0.0)
    part_two = jnp.maximum(shifted - 2.0, 0.0)
    part_three = jnp.maximum(shifted - 3.0, 0.0)
    basis_value = (part_zero**3 - 4.0 * part_one**3 + 6.0 * part_two**3 - 4.0 * part_three**3) / 6.0
    slope_value = (
        part_zero * part_zero
        - 4.0 * part_one * part_one
        + 6.0 * part_two * part_two
        - 4.0 * part_three * part_three
    ) * (0.5 / spacing)
    return (jnp.where(inside, basis_value, 0.0), jnp.where(inside, slope_value, 0.0))


def smooth_penalty(values):
    curvature = values[..., :-2, :] - 2.0 * values[..., 1:-1, :] + values[..., 2:, :]
    padding = [(0, 0)] * (values.ndim - 2) + [(2, 2), (0, 0)]
    padded = jnp.pad(curvature, padding)
    return padded[..., :-2, :] - 2.0 * padded[..., 1:-1, :] + padded[..., 2:, :]


def on_device(inputs, out_grad, route, coef, first_moment, second_moment):
    row_count = inputs.shape[0]
    groups = lax.axis_size("expert")
    members = lax.axis_size("dp")
    experts = groups // SPLIT
    capacity = min(row_count, max(row_count // 16, 2 * row_count // experts))
    slot_count = groups * capacity
    quarter = IN // members
    expert_of = route[:, 0]
    expert_ids = jnp.arange(experts, dtype=jnp.int32)
    chosen = (expert_of[:, None] == expert_ids[None, :]).astype(jnp.int32)
    before = jnp.cumsum(chosen, axis=0) - chosen
    position = jnp.sum(before * chosen, axis=1)
    dispatch = (
        (expert_of[None, None, :] == expert_ids[:, None, None])
        & (position[None, None, :] == jnp.arange(capacity, dtype=jnp.int32)[None, :, None])
    ).astype(jnp.bfloat16)
    sent_inputs = jnp.einsum(
        "ecr,ri->eci", dispatch, inputs, preferred_element_type=jnp.float32
    ).astype(jnp.bfloat16)
    sent_inputs = jnp.broadcast_to(sent_inputs[:, None], (experts, SPLIT, capacity, IN)).reshape(
        groups, capacity, IN
    )
    sent_grads = jnp.einsum(
        "ecr,rsk->esck",
        dispatch,
        out_grad.reshape(row_count, SPLIT, COLS),
        preferred_element_type=jnp.float32,
    ).astype(jnp.bfloat16)
    sent_grads = sent_grads.reshape(groups, capacity, COLS)
    slot_inputs, slot_grads = (
        lax.all_to_all(sent_inputs, "expert", split_axis=0, concat_axis=0, tiled=True),
        lax.all_to_all(sent_grads, "expert", split_axis=0, concat_axis=0, tiled=True),
    )
    slot_inputs = slot_inputs.reshape(slot_count, IN)
    slot_grads = slot_grads.reshape(slot_count, COLS)
    values, slopes = spline_bases(slot_inputs.astype(jnp.float32))
    basis_flat = values.astype(jnp.bfloat16).reshape(slot_count, IN * NB)
    product = jnp.einsum("sa,so->ao", basis_flat, slot_grads, preferred_element_type=jnp.float32)
    grad_owned = lax.psum_scatter(
        product.reshape(quarter * lax.axis_size("dp"), NB, COLS).astype(jnp.bfloat16),
        "dp",
        scatter_dimension=0,
        tiled=True,
    ).astype(jnp.float32)
    coef_piece = lax.all_gather(coef, "dp", axis=1, tiled=True)
    piece_rows = coef_piece.shape[1]
    weight_flat = coef_piece.reshape(piece_rows * NB, COLS)
    projected = jnp.einsum("so,ao->sa", slot_grads, weight_flat, preferred_element_type=jnp.float32)
    projected = projected.reshape(slot_count, piece_rows, NB)
    partial_dx = jnp.sum(projected * slopes, axis=2).astype(jnp.bfloat16)
    returned = lax.all_to_all(
        partial_dx.reshape(groups, capacity, IN), "expert", split_axis=0, concat_axis=0, tiled=True
    )
    summed = jnp.sum(returned.reshape(experts, SPLIT, capacity, IN).astype(jnp.float32), axis=1)
    input_grad = jnp.einsum(
        "ecr,eci->ri", dispatch.astype(jnp.float32), summed, precision=lax.Precision.HIGHEST
    ).astype(jnp.bfloat16)
    coef_float = coef[0].astype(jnp.float32)
    gradient = grad_owned + PENALTY * smooth_penalty(coef_float)
    moment_one = BETA_ONE * first_moment[0].astype(jnp.float32) + (1.0 - BETA_ONE) * gradient
    moment_two = (
        BETA_TWO * second_moment[0].astype(jnp.float32) + (1.0 - BETA_TWO) * gradient * gradient
    )
    update = moment_one / BIAS_ONE / (jnp.sqrt(moment_two / BIAS_TWO) + EPSILON)
    new_coef = coef_float - LEARN_RATE * (update + WEIGHT_DECAY * coef_float)
    return (
        input_grad,
        new_coef[None].astype(jnp.bfloat16),
        moment_one[None].astype(jnp.bfloat16),
        moment_two[None].astype(jnp.bfloat16),
    )


def solution(mesh):
    placed = (
        P(("expert", "dp"), None),
        P(("expert", "dp"), None),
        P(("expert", "dp"), None),
        P("expert", "dp", None, None),
        P("expert", "dp", None, None),
        P("expert", "dp", None, None),
    )
    return jax.shard_map(
        on_device,
        mesh=mesh,
        in_specs=placed,
        out_specs=(
            P(("expert", "dp"), None),
            P("expert", "dp", None, None),
            P("expert", "dp", None, None),
            P("expert", "dp", None, None),
        ),
        check_vma=False,
    )
```

profile of v0, /device:TPU:1, one launch (start us, length us, event | category | flops | bytes accessed | tf_op | source)
XLA Modules:
  0.0 147.5 jit_solution(16368304785161281046)
XLA Ops:
  7.2 0.0 copy-start
  7.2 0.0 copy-start.3
  7.2 0.7 iota_compare_fusion.1
  7.9 0.7 fusion.53
  8.7 0.2 reduce_window_sum.11
  8.8 0.8 select_reduce_fusion
  9.7 0.0 copy-done
  9.7 0.2 convolution_convert_fusion.1
  9.9 0.8 broadcast_in_dim.4
  10.7 18.4 %all-to-all-start.1 = ((bf16[128,8,256]{2,1,0:T(8,128)(2,1)}), bf16[128,8,256]{2,1,0:T(8,128)(2,1)S(1)}, u32[]{:S(2)}, u32[]{:S(2)}) async-start(bf16[128,8,256]{2,1,0:T(8,128)(2,1)} %bitcast.9), calls=%async_computation.1 | async-start | bytes 1048576 | tf_op jit(solution)/shard_map/all_to_all | solution.py:81
  29.2 0.0 all-gather.2.cloned.1.call-start
  29.2 2.0 %bitcast_convert_fusion = (f32[64,8,512]{2,0,1:T(8,128)S(1)}, bf16[1,64,8,512]{3,1,2,0:T(8,128)(2,1)}) fusion(bf16[1,64,8,512]{3,2,1,0:T(8,128)(2,1)} %param.9), kind=kLoop, calls=%fused_computation.68 | loop fusion | flops 262144 | bytes 2097152 | tf_op jit(solution)/shard_map/convert_element_type | solution.py:108
  31.2 0.0 all-gather.2.cloned.1.call-update
  31.3 0.0 copy-done.3
  31.3 1.4 convolution_convert_fusion
  32.7 17.0 %all-to-all-done.1 = bf16[128,8,256]{2,1,0:T(8,128)(2,1)S(1)} async-done(((bf16[128,8,256]{2,1,0:T(8,128)(2,1)}), bf16[128,8,256]{2,1,0:T(8,128)(2,1)S(1)}, u32[]{:S(2)}, u32[]{:S(2)}) %all-to-all-start.1) | async-done | bytes 524320 | tf_op jit(solution)/shard_map/all_to_all | solution.py:81
  49.7 6.4 %all-to-all-start = ((bf16[128,8,512]{2,1,0:T(8,128)(2,1)}), bf16[128,8,512]{2,1,0:T(8,128)(2,1)}, u32[]{:S(2)}, u32[]{:S(2)}) async-start(bf16[128,8,512]{2,1,0:T(8,128)(2,1)} %bitcast.4), calls=%async_computation | async-start | bytes 2097152 | tf_op jit(solution)/shard_map/all_to_all | solution.py:82
  56.2 0.2 reduce-scatter.2.cloned.1.call-start
  56.4 0.1 sub.84
  56.5 0.1 multiply_bitcast_fusion
  56.7 0.3 copy.48
  57.0 8.9 %fusion.25 = bf16[256,8,1024]{2,1,0:T(8,128)(2,1)} fusion(f32[1024,256]{0,1:T(8,128)S(1)} %copy.48, f32[2048]{0:T(1024)S(1)} %sub.84), kind=kLoop, calls=%fused_computation.34 | loop fusion | flops 54525952 | bytes 5251072 | tf_op jit(solution)/shard_map/sa,so->ao/dot_general | solution.py:88
  65.9 20.4 %all-to-all-done = bf16[128,8,512]{2,1,0:T(8,128)(2,1)} async-done(((bf16[128,8,512]{2,1,0:T(8,128)(2,1)}), bf16[128,8,512]{2,1,0:T(8,128)(2,1)}, u32[]{:S(2)}, u32[]{:S(2)}) %all-to-all-start) | async-done | bytes 1048608 | tf_op jit(solution)/shard_map/all_to_all | solution.py:82
  86.2 9.2 %fusion.29 = bf16[256,8,512]{2,0,1:T(8,128)(2,1)} fusion(bf16[256,8,1024]{2,1,0:T(8,128)(2,1)} %fusion.25, bf16[128,8,512]{2,1,0:T(8,128)(2,1)} %all-to-all-done), kind=kOutput, calls=%fused_computation.38 | convolution fusion | flops 2148532224 | bytes 7340032 | tf_op jit(solution)/shard_map/sa,so->ao/dot_general | solution.py:88
  95.4 0.0 reduce-scatter.2.cloned.1.call-update
  95.5 0.0 all-gather.2.cloned.1.call-done
  95.5 9.7 %fusion.6 = bf16[1024,256]{1,0:T(8,128)(2,1)} fusion(f32[1024,256]{1,0:T(8,128)S(1)} %multiply_bitcast_fusion, bf16[1,256,8,512]{3,1,2,0:T(8,128)(2,1)} %all-gather.2.cloned.1.call-done, bf16[128,8,512]{2,1,0:T(8,128)(2,1)} %all-to-all-done), kind=kOutput, calls=%fused_computation.13 | convolution fusion | flops 2195456000 | bytes 4718592 | tf_op jit(solution)/shard_map/so,ao->sa/dot_general | solution.py:98
  105.2 0.0 copy-start.2
  105.2 6.8 %all-to-all-start.2 = ((bf16[128,8,256]{2,1,0:T(8,128)(2,1)}), bf16[128,8,256]{2,1,0:T(8,128)(2,1)S(1)}, u32[]{:S(2)}, u32[]{:S(2)}) async-start(bf16[128,8,256]{2,1,0:T(8,128)(2,1)} %bitcast.103), calls=%async_computation.2 | async-start | bytes 1048576 | tf_op jit(solution)/shard_map/all_to_all | solution.py:101
  112.1 0.0 copy-start.1
  112.1 0.1 slice_add_fusion
  112.2 20.4 %all-to-all-done.2 = bf16[128,8,256]{2,1,0:T(8,128)(2,1)S(1)} async-done(((bf16[128,8,256]{2,1,0:T(8,128)(2,1)}), bf16[128,8,256]{2,1,0:T(8,128)(2,1)S(1)}, u32[]{:S(2)}, u32[]{:S(2)}) %all-to-all-start.2) | async-done | bytes 524320 | tf_op jit(solution)/shard_map/all_to_all | solution.py:101
  132.7 0.1 convert_reduce_fusion
  132.7 0.9 fusion.32
  133.7 0.0 reduce-scatter.2.cloned.1.call-done
  133.7 0.0 copy-done.2
  133.7 1.5 fusion.44
  135.2 1.1 copy.44
  136.2 0.0 copy-done.1
  136.2 2.2 %fusion.45 = (bf16[1,64,8,512]{3,1,2,0:T(8,128)(2,1)S(1)}, bf16[1,64,8,512]{3,1,2,0:T(8,128)(2,1)S(1)}) fusion(f32[64,8,512]{2,0,1:T(8,128)S(1)} %get-tuple-element.17, bf16[1,64,8,512]{3,2,1,0:T(8,128)(2,1)} %param.10, bf16[1,64,8,512]{3,2,1,0:T(8,128)(2,1)S(1)} %copy-done.2, bf16[1,64,8,512]{3,2,1,0:T(8,128)(2,1)S(1)} %copy-done.1), kind=kLoop, calls=%fused_computation.65 | loop fusion | flops 5242880 | bytes 3670016 | tf_op jit(solution)/shard_map/convert_element_type | solution.py:119
  138.5 1.1 copy.43
  139.6 1.1 copy.42
  (3 shorter events, 0.1 us)
Async XLA Ops:
  7.2 2.5 %copy-start = (bf16[128,256]{1,0:T(8,128)(2,1)S(1)}, bf16[128,256]{1,0:T(8,128)(2,1)}, u32[]{:S(2)}) copy-start(bf16[128,256]{1,0:T(8,128)(2,1)} %param.6) | copy-start | bytes 196612
  7.2 24.1 %copy-start.3 = (bf16[128,2048]{1,0:T(8,128)(2,1)S(1)}, bf16[128,2048]{1,0:T(8,128)(2,1)}, u32[]{:S(2)}) copy-start(bf16[128,2048]{1,0:T(8,128)(2,1)} %param.7) | copy-start | bytes 1572868
  10.7 39.0 %all-to-all-start.1 = ((bf16[128,8,256]{2,1,0:T(8,128)(2,1)}), bf16[128,8,256]{2,1,0:T(8,128)(2,1)S(1)}, u32[]{:S(2)}, u32[]{:S(2)}) async-start(bf16[128,8,256]{2,1,0:T(8,128)(2,1)} %bitcast.9), calls=%async_computation.1 | async-start | bytes 1048576 | tf_op jit(solution)/shard_map/all_to_all | solution.py:81
  29.2 66.3 %all-gather.2.cloned.1.call-start = ((), (), s32[]{:S(2)}) async-start(), calls=%async_computation.4 | async-start | bytes 2621440 | tf_op jit(solution)/shard_map/all_gather | solution.py:95
  49.7 36.5 %all-to-all-start = ((bf16[128,8,512]{2,1,0:T(8,128)(2,1)}), bf16[128,8,512]{2,1,0:T(8,128)(2,1)}, u32[]{:S(2)}, u32[]{:S(2)}) async-start(bf16[128,8,512]{2,1,0:T(8,128)(2,1)} %bitcast.4), calls=%async_computation | async-start | bytes 2097152 | tf_op jit(solution)/shard_map/all_to_all | solution.py:82
  56.2 77.5 %reduce-scatter.2.cloned.1.call-start = ((), (), s32[]{:S(2)}) async-start(), calls=%async_computation.5 | async-start | bytes 2621440 | tf_op jit(solution)/shard_map/reduce_scatter | solution.py:89
  105.2 28.5 %copy-start.2 = (bf16[1,64,8,512]{3,2,1,0:T(8,128)(2,1)S(1)}, bf16[1,64,8,512]{3,2,1,0:T(8,128)(2,1)}, u32[]{:S(2)}) copy-start(bf16[1,64,8,512]{3,2,1,0:T(8,128)(2,1)} %param.11) | copy-start | bytes 1572868
  105.2 27.4 %all-to-all-start.2 = ((bf16[128,8,256]{2,1,0:T(8,128)(2,1)}), bf16[128,8,256]{2,1,0:T(8,128)(2,1)S(1)}, u32[]{:S(2)}, u32[]{:S(2)}) async-start(bf16[128,8,256]{2,1,0:T(8,128)(2,1)} %bitcast.103), calls=%async_computation.2 | async-start | bytes 1048576 | tf_op jit(solution)/shard_map/all_to_all | solution.py:101
  112.1 24.2 %copy-start.1 = (bf16[1,64,8,512]{3,2,1,0:T(8,128)(2,1)S(1)}, bf16[1,64,8,512]{3,2,1,0:T(8,128)(2,1)}, u32[]{:S(2)}) copy-start(bf16[1,64,8,512]{3,2,1,0:T(8,128)(2,1)} %param.9) | copy-start | bytes 1572868
Sparse Core Ops, SparseCore 0:
  32.7 36.9 all-gather.1
  95.6 28.5 reduce-scatter.1
where the time goes:
time: 148 us
  waiting for transfers between devices  57.9 us (39%)
  starting transfers between devices  32 us (22%)
  matrix products  21.5 us (15%)
  other arithmetic  17.4 us (12%)
  between operations  14.2 us (10%)
  local copies, waits for them, and re-layouts  4.56 us (3%)
    all_to_all x1, waiting for transfers between devices, on_device(): lax.all_to_all(partial_dx.reshape(groups, capacity, IN), 'expert', split_...  20.4 us
    all_to_all x1, waiting for transfers between devices, on_device(): lax.all_to_all(sent_grads, 'expert', split_axis=0, concat_axis=0, tiled=T...  20.4 us
    all_to_all x1, starting transfers between devices, on_device(): lax.all_to_all(sent_inputs, 'expert', split_axis=0, concat_axis=0, tiled=...  18.4 us
    all_to_all x1, waiting for transfers between devices, on_device(): lax.all_to_all(sent_inputs, 'expert', split_axis=0, concat_axis=0, tiled=...  17 us
    dot_general x1, matrix products, on_device(): jnp.einsum('so,ao->sa', slot_grads, weight_flat, preferred_element_type=j...  9.74 us
    dot_general x1, matrix products, on_device(): jnp.einsum('sa,so->ao', basis_flat, slot_grads, preferred_element_type=jn...  9.19 us
    dot_general x1, other arithmetic, on_device(): jnp.einsum('sa,so->ao', basis_flat, slot_grads, preferred_element_type=jn...  8.86 us
    all_to_all x1, starting transfers between devices, on_device(): lax.all_to_all(partial_dx.reshape(groups, capacity, IN), 'expert', split_...  6.85 us
  transfers between devices with their start and end apart: 5, of which 3 were waited for; matrix products, arithmetic and copies ran while one was open for 22% of the time, Pallas kernels for 0%

commit v1 on v0

v1 whole, which is shorter than its diff:
```python
import functools

import jax
import jax.numpy as jnp
from jax import lax
from jax.experimental import pallas as pl
from jax.experimental.pallas import tpu as pltpu
from jax.sharding import PartitionSpec as P

IN = 256
NB = 8
SPLIT = 4
COLS = 512
CAP = 8
ROWS = 128
LANES = 128
WIDTH = COLS + IN

PENALTY = 10.0
LEARN_RATE = 0.001
BETA_ONE = 0.9
BETA_TWO = 0.999
EPSILON = 1e-08
WEIGHT_DECAY = 0.1
BIAS_ONE = 0.999973438601112
BIAS_TWO = 0.0952078528855534
HALF_INV_SPACING = 0.625

f32 = jnp.float32
bf16 = jnp.bfloat16


def vmem(n):
    return [pl.BlockSpec(memory_space=pltpu.VMEM) for _ in range(n)]


def slot_matrix(route_row, slots):
    wide = jnp.broadcast_to(route_row.astype(f32), (ROWS, ROWS))
    tall = jnp.transpose(wide)
    earlier = lax.broadcasted_iota(jnp.int32, (ROWS, ROWS), 0) < lax.broadcasted_iota(
        jnp.int32, (ROWS, ROWS), 1
    )
    rank = jnp.sum(jnp.where((wide == tall) & earlier, 1.0, 0.0), axis=0, keepdims=True)
    slot = route_row * CAP + rank.astype(jnp.int32)
    hit = lax.broadcasted_iota(jnp.int32, (slots, ROWS), 0) == slot
    return jnp.where(hit, 1.0, 0.0).astype(bf16)


def dispatch_kernel(route_ref, inputs_ref, grads_ref, send_ref, onehot_ref):
    experts = send_ref.shape[0]
    onehot = slot_matrix(route_ref[...], experts * CAP)
    onehot_ref[...] = onehot
    sent = jnp.dot(onehot, inputs_ref[...], preferred_element_type=f32).astype(bf16)
    sent = sent.reshape(experts, CAP, IN)
    for s in range(SPLIT):
        block = jnp.dot(
            onehot, grads_ref[:, s * COLS : (s + 1) * COLS], preferred_element_type=f32
        ).astype(bf16)
        send_ref[:, s, :, 0:COLS] = block.reshape(experts, CAP, COLS)
        send_ref[:, s, :, COLS:WIDTH] = sent


def dispatch(route_row, inputs, out_grad, experts):
    return pl.pallas_call(
        dispatch_kernel,
        out_shape=(
            jax.ShapeDtypeStruct((experts, SPLIT, CAP, WIDTH), bf16),
            jax.ShapeDtypeStruct((experts * CAP, ROWS), bf16),
        ),
        in_specs=vmem(3),
        out_specs=tuple(vmem(2)),
        name="dispatch",
    )(route_row, inputs, out_grad)


def relayout_kernel(coef_ref, out_ref, wide_ref):
    quarter = out_ref.shape[1]
    for j in range(COLS // LANES):
        at = slice(j * LANES, (j + 1) * LANES)
        wide_ref[j] = coef_ref[:, :, at].reshape(quarter * NB, LANES).astype(f32)
        for k in range(NB):
            out_ref[k, :, at] = wide_ref[j, pl.ds(k, quarter, stride=NB), :].astype(bf16)


def relayout(coef):
    quarter = coef.shape[0]
    return pl.pallas_call(
        relayout_kernel,
        out_shape=jax.ShapeDtypeStruct((NB, quarter, COLS), bf16),
        in_specs=vmem(1),
        out_specs=vmem(1)[0],
        scratch_shapes=[pltpu.VMEM((COLS // LANES, quarter * NB, LANES), f32)],
        name="relayout",
    )(coef)


def cells(x):
    t = x.astype(f32) * 1.25 + 5.5
    cell = jnp.floor(t)
    return cell, t - cell


def pick(cell, k, pieces):
    out = jnp.where(cell == float(k + 3), pieces[3], 0.0)
    for j in (2, 1, 0):
        out = jnp.where(cell == float(k + j), pieces[j], out)
    return out


def project_kernel(data_ref, coef_ref, partial_ref, turned_ref):
    x = data_ref[:, COLS:WIDTH]
    cell, f = cells(x)
    g = 1.0 - f
    c = HALF_INV_SPACING
    pieces = (
        c * f * f,
        c + f * (2.0 * c - 3.0 * c * f),
        -c - g * (2.0 * c - 3.0 * c * g),
        -c * g * g,
    )
    grads = data_ref[:, 0:COLS]
    total = None
    for k in range(NB):
        projected = lax.dot_general(
            grads, coef_ref[k], (((1,), (1,)), ((), ())), preferred_element_type=f32
        )
        term = projected * pick(cell, k, pieces)
        total = term if total is None else total + term
    partial_ref[...] = total.astype(bf16)
    turned_ref[...] = jnp.transpose(x.astype(f32)).astype(bf16)


def project(data, coef_all):
    slots = data.shape[0]
    step = 256
    return pl.pallas_call(
        project_kernel,
        grid=(slots // step,),
        out_shape=(
            jax.ShapeDtypeStruct((slots, IN), bf16),
            jax.ShapeDtypeStruct((IN, slots), bf16),
        ),
        in_specs=[
            pl.BlockSpec((step, WIDTH), lambda i: (i, 0)),
            pl.BlockSpec((NB, IN, COLS), lambda i: (0, 0, 0)),
        ],
        out_specs=(
            pl.BlockSpec((step, IN), lambda i: (i, 0)),
            pl.BlockSpec((IN, step), lambda i: (0, i)),
        ),
        name="project",
    )(data, coef_all)


def gradient_kernel(first_ref, turned_ref, data_ref, *refs):
    outs, basis_ref = refs[:-1], refs[-1]
    quarter = turned_ref.shape[0] // len(outs)
    for turn, out_ref in enumerate(outs):
        start = lax.rem(first_ref[0] + turn, len(outs)) * quarter
        x = turned_ref[pl.ds(pl.multiple_of(start, quarter), quarter), :]
        cell, f = cells(x)
        g = 1.0 - f
        c = 1.0 / 6.0
        pieces = (
            c * f * f * f,
            c + f * (0.5 + f * (0.5 - 0.5 * f)),
            c + g * (0.5 + g * (0.5 - 0.5 * g)),
            c * g * g * g,
        )
        for k in range(NB):
            basis_ref[turn % 2, k * quarter : (k + 1) * quarter, :] = pick(cell, k, pieces).astype(bf16)
        out_ref[...] = (
            jnp.dot(basis_ref[turn % 2], data_ref[...], preferred_element_type=f32)
            .astype(bf16)
            .reshape(out_ref.shape)
        )


def gradient(first, turned, data, members):
    quarter = IN // members
    slots = data.shape[0]
    return pl.pallas_call(
        gradient_kernel,
        grid=(1,),
        out_shape=tuple(jax.ShapeDtypeStruct((NB, quarter, COLS), bf16) for _ in range(members)),
        in_specs=[
            pl.BlockSpec(memory_space=pltpu.SMEM),
            pl.BlockSpec((IN, slots), lambda i: (0, 0)),
            pl.BlockSpec((slots, COLS), lambda i: (0, 0)),
        ],
        out_specs=tuple(pl.BlockSpec((NB, quarter, COLS), lambda i: (0, 0, 0)) for _ in range(members)),
        scratch_shapes=[pltpu.VMEM((2, NB * quarter, slots), bf16)],
        name="gradient",
    )(first, turned, data)


def adam_kernel(*refs):
    parts = refs[: len(refs) - 7]
    coef_ref, one_ref, two_ref, new_ref, one_out, two_out, wide_ref = refs[len(refs) - 7 :]
    rows = coef_ref.shape[0]
    for k in range(NB):
        piece = parts[0][k].astype(f32)
        for part in parts[1:]:
            piece = piece + part[k].astype(f32)
        for j in range(COLS // LANES):
            wide_ref[j, pl.ds(k, rows, stride=NB), :] = piece[:, j * LANES : (j + 1) * LANES]
    grad = jnp.concatenate(
        [wide_ref[j].reshape(rows, NB, LANES) for j in range(COLS // LANES)], axis=2
    )
    c = coef_ref[...].astype(f32)
    k = lax.broadcasted_iota(jnp.int32, (1, NB, COLS), 1)

    def row(values):
        out = jnp.full((1, NB, COLS), float(values[0]), f32)
        for index in range(1, NB):
            if values[index] != values[0]:
                out = jnp.where(k == index, float(values[index]), out)
        return out

    pen = c * row((1, 5, 6, 6, 6, 6, 5, 1))
    pen = pen + pltpu.roll(c, 1, 1) * row((0, -2, -4, -4, -4, -4, -4, -2))
    pen = pen + pltpu.roll(c, NB - 1, 1) * row((-2, -4, -4, -4, -4, -4, -2, 0))
    pen = pen + pltpu.roll(c, 2, 1) * row((0, 0, 1, 1, 1, 1, 1, 1))
    pen = pen + pltpu.roll(c, NB - 2, 1) * row((1, 1, 1, 1, 1, 1, 0, 0))
    gradient_all = grad + PENALTY * pen
    one = BETA_ONE * one_ref[...].astype(f32) + (1.0 - BETA_ONE) * gradient_all
    two = BETA_TWO * two_ref[...].astype(f32) + (1.0 - BETA_TWO) * gradient_all * gradient_all
    update = one * (1.0 / BIAS_ONE) / (jnp.sqrt(two * (1.0 / BIAS_TWO)) + EPSILON)
    new_ref[...] = (c - LEARN_RATE * (update + WEIGHT_DECAY * c)).astype(bf16)
    one_out[...] = one.astype(bf16)
    two_out[...] = two.astype(bf16)


def adam(parts, coef, one, two):
    quarter = coef.shape[0]
    step = 16
    major = pl.BlockSpec((NB, step, COLS), lambda i: (0, i, 0))
    state = pl.BlockSpec((step, NB, COLS), lambda i: (i, 0, 0))
    return pl.pallas_call(
        adam_kernel,
        grid=(quarter // step,),
        out_shape=tuple(jax.ShapeDtypeStruct(coef.shape, bf16) for _ in range(3)),
        in_specs=[major] * len(parts) + [state] * 3,
        out_specs=(state,) * 3,
        scratch_shapes=[pltpu.VMEM((COLS // LANES, step * NB, LANES), f32)],
        name="adam",
    )(*parts, coef, one, two)


def combine_kernel(returned_ref, onehot_ref, out_ref):
    experts = returned_ref.shape[0]
    total = returned_ref[:, 0].astype(f32)
    for s in range(1, SPLIT):
        total = total + returned_ref[:, s].astype(f32)
    total = total.astype(bf16).reshape(experts * CAP, IN)
    out_ref[...] = lax.dot_general(
        onehot_ref[...], total, (((0,), (0,)), ((), ())), preferred_element_type=f32
    ).astype(bf16)


def combine(returned, onehot):
    return pl.pallas_call(
        combine_kernel,
        out_shape=jax.ShapeDtypeStruct((ROWS, IN), bf16),
        in_specs=vmem(2),
        out_specs=vmem(1)[0],
        name="combine",
    )(returned, onehot)


def on_device(inputs, out_grad, route, coef, first_moment, second_moment):
    groups = lax.axis_size("expert")
    members = lax.axis_size("dp")
    experts = groups // SPLIT
    here = lax.axis_index("dp")
    quarter = IN // members

    def shift(value, by):
        return lax.ppermute(value, "dp", [(i, (i + by) % members) for i in range(members)])

    send, onehot = dispatch(route.reshape(1, ROWS), inputs, out_grad, experts)
    got = lax.all_to_all(
        send.reshape(groups, CAP, WIDTH), "expert", split_axis=0, concat_axis=0, tiled=True
    ).reshape(groups * CAP, WIDTH)

    own = relayout(coef[0])
    coef_all = jnp.zeros((NB, IN, COLS), bf16)
    for turn in range(members):
        piece = own if turn == 0 else shift(own, -turn)
        at = lax.rem(here + turn, members) * quarter
        coef_all = lax.dynamic_update_slice(coef_all, piece, (0, at, 0))

    partial, turned = project(got, coef_all)
    returned = lax.all_to_all(
        partial.reshape(groups, CAP, IN), "expert", split_axis=0, concat_axis=0, tiled=True
    )
    pieces = gradient(here.reshape(1), turned, got, members)
    parts = [pieces[0]] + [shift(pieces[turn], turn) for turn in range(1, members)]
    new_coef, new_one, new_two = adam(parts, coef[0], first_moment[0], second_moment[0])
    input_grad = combine(returned.reshape(experts, SPLIT, CAP, IN), onehot)
    return input_grad, new_coef[None], new_one[None], new_two[None]


def solution(mesh):
    rows = P(("expert", "dp"), None)
    state = P("expert", "dp", None, None)
    return jax.shard_map(
        on_device,
        mesh=mesh,
        in_specs=(rows, rows, rows, state, state, state),
        out_specs=(rows, state, state, state),
        check_vma=False,
    )
```

time: 148 us -> 126 us (0.85)
  Pallas kernels: 0 us -> 25.4 us
  matrix products: 21.5 us -> 0 us
  other arithmetic: 17.4 us -> 0 us
  starting transfers between devices: 32 us -> 45.9 us
  waiting for transfers between devices: 57.9 us -> 44.3 us
  between operations: 14.2 us -> 0.75 us
  local copies, waits for them, and re-layouts: 4.56 us -> 8.75 us
    all_to_all x3 -> x2, waiting for transfers between devices: 57.8 us -> 5.05 us  [the longest x1 5.05 us: on_device(): lax.all_to_all(send.reshape(groups, CAP, WIDTH), 'expert', split_axis=0,...]
    ppermute x0 -> x6, waiting for transfers between devices: none -> 39.2 us  [shift(): lax.ppermute(value, 'dp', [(i, (i + by) % members) for i in range(members)])]
    pallas_call x0 -> x6, Pallas kernels: none -> 25.4 us  [the longest x1 6.74 us: project(): pl.pallas_call(project_kernel, grid=(slots // step,), out_shape=(jax.Shap...]
    dot_general x5 -> x0, matrix products: 21.5 us -> none  [the longest x1 9.74 us: on_device(): jnp.einsum('so,ao->sa', slot_grads, weight_flat, preferred_element_type=j...]
    ppermute x0 -> x6, starting transfers between devices: none -> 18.7 us  [shift(): lax.ppermute(value, 'dp', [(i, (i + by) % members) for i in range(members)])]
    dot_general x1 -> x0, other arithmetic: 8.86 us -> none  [on_device(): jnp.einsum('sa,so->ao', basis_flat, slot_grads, preferred_element_type=jn...]
    convert_element_type x4 -> x0, other arithmetic: 6.48 us -> none  [the longest x1 2.25 us: on_device(): moment_one[None].astype(jnp.bfloat16)]
    dynamic_update_slice x0 -> x4, local copies, waits for them, and re-layouts: none -> 4.49 us  [on_device(): coef_all = lax.dynamic_update_slice(coef_all, piece, (0, at, 0))]
  transfers between devices with their start and end apart: 5 -> 8, of which waited for: 3 -> 7; matrix products, arithmetic and copies ran while one was open for 22% -> 5% of each run, Pallas kernels for 0% -> 11%
where the time goes in v1:
time: 126 us; the launch traced here: 125 us
  starting transfers between devices  45.9 us (36%)
  waiting for transfers between devices  44.3 us (35%)
  Pallas kernels  25.4 us (20%)
  local copies, waits for them, and re-layouts  8.75 us (7%)
    ppermute x6, waiting for transfers between devices, shift(): lax.ppermute(value, 'dp', [(i, (i + by) % members) for i in range(members)])  39.2 us
    ppermute x6, starting transfers between devices, shift(): lax.ppermute(value, 'dp', [(i, (i + by) % members) for i in range(members)])  18.7 us
    all_to_all x1, starting transfers between devices, on_device(): lax.all_to_all(send.reshape(groups, CAP, WIDTH), 'expert', split_axis=0,...  18.4 us
    all_to_all x1, starting transfers between devices, on_device(): lax.all_to_all(partial.reshape(groups, CAP, IN), 'expert', split_axis=0,...  8.82 us
    pallas_call x1, Pallas kernels, project(): pl.pallas_call(project_kernel, grid=(slots // step,), out_shape=(jax.Shap...  6.74 us
    pallas_call x1, Pallas kernels, gradient(): pl.pallas_call(gradient_kernel, grid=(1,), out_shape=tuple((jax.ShapeDtyp...  6.46 us
    pallas_call x1, Pallas kernels, adam(): pl.pallas_call(adam_kernel, grid=(quarter // step,), out_shape=tuple((jax...  5.42 us
    all_to_all x1, waiting for transfers between devices, on_device(): lax.all_to_all(send.reshape(groups, CAP, WIDTH), 'expert', split_axis=0,...  5.05 us
  transfers between devices with their start and end apart: 8, of which 7 were waited for; matrix products, arithmetic and copies ran while one was open for 5% of the time, Pallas kernels for 11%

profile of v1, /device:TPU:1, one launch (start us, length us, event | category | flops | bytes accessed | tf_op | source)
XLA Modules:
  0.0 125.1 jit_solution(1214909150537235320)
XLA Ops:
  0.6 2.8 %dispatch.1 = (bf16[32,4,8,768]{3,2,1,0:T(8,128)(2,1)}, bf16[256,128]{1,0:T(8,128)(2,1)}) custom-call(s32[1,128]{1,0:T(1,128)} %bitcast.21, bf16[128,256]{1,0:T(8,128)(2,1)} %inputs_ref.1, bf16[128,2048]{1,0:T(8,128)(2,1)} %grads_ref.1), custom_call_target="tpu_custom_call" | custom-call | tf_op jit(solution)/shard_map/dispatch/pallas_call | solution.py:64
  3.4 18.4 %all-to-all-start = ((bf16[128,8,768]{2,1,0:T(8,128)(2,1)}), bf16[128,8,768]{2,1,0:T(8,128)(2,1)S(1)}, u32[]{:S(2)}, u32[]{:S(2)}) async-start(bf16[128,8,768]{2,1,0:T(8,128)(2,1)} %bitcast.17), calls=%async_computation | async-start | bytes 3145728 | tf_op jit(solution)/shard_map/all_to_all | solution.py:282
  21.9 2.1 %relayout.1 = bf16[8,64,512]{2,1,0:T(8,128)(2,1)} custom-call(bf16[64,8,512]{2,1,0:T(8,128)(2,1)} %bitcast.14), custom_call_target="tpu_custom_call" | custom-call | tf_op jit(solution)/shard_map/relayout/pallas_call | solution.py:87
  24.0 0.0 copy-start.2
  24.0 4.5 %collective-permute-start = (bf16[8,64,512]{2,1,0:T(8,128)(2,1)}, bf16[8,64,512]{2,1,0:T(8,128)(2,1)}, u32[]{:S(2)}, u32[]{:S(2)}) collective-permute-start(bf16[8,64,512]{2,1,0:T(8,128)(2,1)} %relayout.1), channel_id=1, source_target_pairs={{0,3},{1,0},{2,1},{3,2},{4,7},{5,4},{6,5},{7,6},{8,11},{9,8},{10,9... | collective-permute-start | bytes 1572872 | tf_op jit(solution)/shard_map/ppermute | solution.py:279
  28.5 2.4 %collective-permute-start.1 = (bf16[8,64,512]{2,1,0:T(8,128)(2,1)}, bf16[8,64,512]{2,1,0:T(8,128)(2,1)S(1)}, u32[]{:S(2)}, u32[]{:S(2)}) collective-permute-start(bf16[8,64,512]{2,1,0:T(8,128)(2,1)} %relayout.1), channel_id=1, source_target_pairs={{0,2},{1,3},{2,0},{3,1},{4,6},{5,7},{6,4},{7,5},{8,10},{9,11},{10,... | collective-permute-start | bytes 1572872 | tf_op jit(solution)/shard_map/ppermute | solution.py:279
  30.9 2.5 %collective-permute-start.2 = (bf16[8,64,512]{2,1,0:T(8,128)(2,1)}, bf16[8,64,512]{2,1,0:T(8,128)(2,1)S(1)}, u32[]{:S(2)}, u32[]{:S(2)}) collective-permute-start(bf16[8,64,512]{2,1,0:T(8,128)(2,1)} %relayout.1), channel_id=1, source_target_pairs={{0,1},{1,2},{2,3},{3,0},{4,5},{5,6},{6,7},{7,4},{8,9},{9,10},{10,1... | collective-permute-start | bytes 1572872 | tf_op jit(solution)/shard_map/ppermute | solution.py:279
  33.5 1.5 %broadcast_in_dim.12 = bf16[8,256,512]{2,1,0:T(8,128)(2,1)} broadcast(bf16[]{:T(256)} %constant.9.clone.1), dimensions={} | broadcast | bytes 2097154 | tf_op jit(solution)/shard_map/broadcast_in_dim | solution.py:287
  35.0 0.0 copy-done.2
  35.0 0.9 constant_dynamic-update-slice_fusion.3
  35.9 4.1 %collective-permute-done = bf16[8,64,512]{2,1,0:T(8,128)(2,1)} collective-permute-done((bf16[8,64,512]{2,1,0:T(8,128)(2,1)}, bf16[8,64,512]{2,1,0:T(8,128)(2,1)}, u32[]{:S(2)}, u32[]{:S(2)}) %collective-permute-start) | collective-permute-done | bytes 524320 | tf_op jit(solution)/shard_map/ppermute | solution.py:279
  39.9 1.9 %constant_dynamic-update-slice_fusion.2 = bf16[8,256,512]{2,1,0:T(8,128)(2,1)} fusion(bf16[8,256,512]{2,1,0:T(8,128)(2,1)} %constant_dynamic-update-slice_fusion.3, bf16[8,64,512]{2,1,0:T(8,128)(2,1)} %collective-permute-done, s32[]{:T(128)S(6)} %select_n.13), kind=kLoop, calls=%fused_computation.2 | loop fusion | bytes 1048580 | tf_op jit(solution)/shard_map/dynamic_update_slice | solution.py:291
  41.8 2.6 %collective-permute-done.1 = bf16[8,64,512]{2,1,0:T(8,128)(2,1)S(1)} collective-permute-done((bf16[8,64,512]{2,1,0:T(8,128)(2,1)}, bf16[8,64,512]{2,1,0:T(8,128)(2,1)S(1)}, u32[]{:S(2)}, u32[]{:S(2)}) %collective-permute-start.1) | collective-permute-done | bytes 524320 | tf_op jit(solution)/shard_map/ppermute | solution.py:279
  44.4 0.9 constant_dynamic-update-slice_fusion.1
  45.3 11.9 %collective-permute-done.2 = bf16[8,64,512]{2,1,0:T(8,128)(2,1)S(1)} collective-permute-done((bf16[8,64,512]{2,1,0:T(8,128)(2,1)}, bf16[8,64,512]{2,1,0:T(8,128)(2,1)S(1)}, u32[]{:S(2)}, u32[]{:S(2)}) %collective-permute-start.2) | collective-permute-done | bytes 524320 | tf_op jit(solution)/shard_map/ppermute | solution.py:279
  57.2 0.9 constant_dynamic-update-slice_fusion.coef_ref
  58.1 5.0 %all-to-all-done = bf16[128,8,768]{2,1,0:T(8,128)(2,1)S(1)} async-done(((bf16[128,8,768]{2,1,0:T(8,128)(2,1)}), bf16[128,8,768]{2,1,0:T(8,128)(2,1)S(1)}, u32[]{:S(2)}, u32[]{:S(2)}) %all-to-all-start) | async-done | bytes 1572896 | tf_op jit(solution)/shard_map/all_to_all | solution.py:282
  63.1 0.0 copy-start
  63.1 1.1 copy-done
  64.2 6.7 %project.1 = (bf16[1024,256]{1,0:T(8,128)(2,1)}, bf16[256,1024]{1,0:T(8,128)(2,1)}) custom-call(bf16[1024,768]{1,0:T(8,128)(2,1)} %bitcast.12, bf16[8,256,512]{2,1,0:T(8,128)(2,1)} %constant_dynamic-update-slice_fusion.coef_ref), custom_call_target="tpu_custom_call" | custom-call | tf_op jit(solution)/shard_map/project/pallas_call | solution.py:136
  71.0 8.8 %all-to-all-start.1 = ((bf16[128,8,256]{2,1,0:T(8,128)(2,1)}), bf16[128,8,256]{2,1,0:T(8,128)(2,1)S(1)}, u32[]{:S(2)}, u32[]{:S(2)}) async-start(bf16[128,8,256]{2,1,0:T(8,128)(2,1)} %bitcast.20), calls=%async_computation.1 | async-start | bytes 1048576 | tf_op jit(solution)/shard_map/all_to_all | solution.py:294
  79.8 6.5 %gradient.1 = (bf16[8,64,512]{2,1,0:T(8,128)(2,1)}, bf16[8,64,512]{2,1,0:T(8,128)(2,1)}, bf16[8,64,512]{2,1,0:T(8,128)(2,1)}, bf16[8,64,512]{2,1,0:T(8,128)(2,1)}) custom-call(s32[1]{0:T(128)} %bitcast.6.first_ref, bf16[256,1024]{1,0:T(8,128)(2,1)} %get-tuple-element.18.turned_ref, bf16[1024,768]{1,0:T(8,128)(2,1)} %bitcast.13), custom_call_target="tpu_custom_call" | custom-call | tf_op jit(solution)/shard_map/gradient/pallas_call | solution.py:182
  86.3 1.9 %collective-permute-start.3 = (bf16[8,64,512]{2,1,0:T(8,128)(2,1)}, bf16[8,64,512]{2,1,0:T(8,128)(2,1)S(1)}, u32[]{:S(2)}, u32[]{:S(2)}) collective-permute-start(bf16[8,64,512]{2,1,0:T(8,128)(2,1)} %get-tuple-element.20), channel_id=1, source_target_pairs={{0,1},{1,2},{2,3},{3,0},{4,5},{5,6},{6,7},{7,4},{8,9},{9,10},{10,1... | collective-permute-start | bytes 1572872 | tf_op jit(solution)/shard_map/ppermute | solution.py:279
  88.2 4.3 %collective-permute-start.4 = (bf16[8,64,512]{2,1,0:T(8,128)(2,1)}, bf16[8,64,512]{2,1,0:T(8,128)(2,1)S(1)}, u32[]{:S(2)}, u32[]{:S(2)}) collective-permute-start(bf16[8,64,512]{2,1,0:T(8,128)(2,1)} %get-tuple-element.21), channel_id=1, source_target_pairs={{0,2},{1,3},{2,0},{3,1},{4,6},{5,7},{6,4},{7,5},{8,10},{9,11},{10,... | collective-permute-start | bytes 1572872 | tf_op jit(solution)/shard_map/ppermute | solution.py:279
  92.5 3.1 %collective-permute-start.5 = (bf16[8,64,512]{2,1,0:T(8,128)(2,1)}, bf16[8,64,512]{2,1,0:T(8,128)(2,1)S(1)}, u32[]{:S(2)}, u32[]{:S(2)}) collective-permute-start(bf16[8,64,512]{2,1,0:T(8,128)(2,1)} %get-tuple-element.22), channel_id=1, source_target_pairs={{0,3},{1,0},{2,1},{3,2},{4,7},{5,4},{6,5},{7,6},{8,11},{9,8},{10,9... | collective-permute-start | bytes 1572872 | tf_op jit(solution)/shard_map/ppermute | solution.py:279
  95.5 6.9 %collective-permute-done.3.refs_1_ = bf16[8,64,512]{2,1,0:T(8,128)(2,1)S(1)} collective-permute-done((bf16[8,64,512]{2,1,0:T(8,128)(2,1)}, bf16[8,64,512]{2,1,0:T(8,128)(2,1)S(1)}, u32[]{:S(2)}, u32[]{:S(2)}) %collective-permute-start.3) | collective-permute-done | bytes 524320 | tf_op jit(solution)/shard_map/ppermute | solution.py:279
  102.4 0.0 copy-start.3
  102.5 10.6 %collective-permute-done.4.refs_2_ = bf16[8,64,512]{2,1,0:T(8,128)(2,1)S(1)} collective-permute-done((bf16[8,64,512]{2,1,0:T(8,128)(2,1)}, bf16[8,64,512]{2,1,0:T(8,128)(2,1)S(1)}, u32[]{:S(2)}, u32[]{:S(2)}) %collective-permute-start.4) | collective-permute-done | bytes 524320 | tf_op jit(solution)/shard_map/ppermute | solution.py:279
  113.1 0.0 copy-start.4
  113.1 3.1 %collective-permute-done.5.refs_3_ = bf16[8,64,512]{2,1,0:T(8,128)(2,1)S(1)} collective-permute-done((bf16[8,64,512]{2,1,0:T(8,128)(2,1)}, bf16[8,64,512]{2,1,0:T(8,128)(2,1)S(1)}, u32[]{:S(2)}, u32[]{:S(2)}) %collective-permute-start.5) | collective-permute-done | bytes 524320 | tf_op jit(solution)/shard_map/ppermute | solution.py:279
  116.2 0.0 copy-start.5
  116.2 0.0 copy-done.3
  116.3 0.0 copy-done.4
  116.3 0.8 copy-done.5
  117.0 5.4 %adam.1 = (bf16[64,8,512]{2,1,0:T(8,128)(2,1)}, bf16[64,8,512]{2,1,0:T(8,128)(2,1)}, bf16[64,8,512]{2,1,0:T(8,128)(2,1)}) custom-call(bf16[8,64,512]{2,1,0:T(8,128)(2,1)} %get-tuple-element.19.refs_0_, bf16[8,64,512]{2,1,0:T(8,128)(2,1)} %copy-done.3, bf16[8,64,512]{2,1,0:T(8,128)(2,1)} %copy-done.4, bf16[8,64,512]{2,1,0:T(8,128)(2,1)} %copy-done.5, ...), custom_call_target="tpu_custom_call" | custom-call | tf_op jit(solution)/shard_map/adam/pallas_call | solution.py:239
  122.5 0.0 all-to-all-done.1
  122.5 0.0 copy-start.1
  122.5 0.8 copy-done.1
  123.3 1.9 %combine.1 = bf16[128,256]{1,0:T(8,128)(2,1)} custom-call(bf16[32,4,8,256]{3,2,1,0:T(8,128)(2,1)} %bitcast.16, bf16[256,128]{1,0:T(8,128)(2,1)} %get-tuple-element.17.onehot_ref), custom_call_target="tpu_custom_call" | custom-call | tf_op jit(solution)/shard_map/combine/pallas_call | solution.py:262
Async XLA Ops:
  3.4 59.7 %all-to-all-start = ((bf16[128,8,768]{2,1,0:T(8,128)(2,1)}), bf16[128,8,768]{2,1,0:T(8,128)(2,1)S(1)}, u32[]{:S(2)}, u32[]{:S(2)}) async-start(bf16[128,8,768]{2,1,0:T(8,128)(2,1)} %bitcast.17), calls=%async_computation | async-start | bytes 3145728 | tf_op jit(solution)/shard_map/all_to_all | solution.py:282
  24.0 11.0 %copy-start.2 = (bf16[8,64,512]{2,1,0:T(8,128)(2,1)S(1)}, bf16[8,64,512]{2,1,0:T(8,128)(2,1)}, u32[]{:S(2)}) copy-start(bf16[8,64,512]{2,1,0:T(8,128)(2,1)} %relayout.1) | copy-start | bytes 1572868
  24.0 15.9 %collective-permute-start = (bf16[8,64,512]{2,1,0:T(8,128)(2,1)}, bf16[8,64,512]{2,1,0:T(8,128)(2,1)}, u32[]{:S(2)}, u32[]{:S(2)}) collective-permute-start(bf16[8,64,512]{2,1,0:T(8,128)(2,1)} %relayout.1), channel_id=1, source_target_pairs={{0,3},{1,0},{2,1},{3,2},{4,7},{5,4},{6,5},{7,6},{8,11},{9,8},{10,9... | collective-permute-start | bytes 1572872 | tf_op jit(solution)/shard_map/ppermute | solution.py:279
  28.5 15.9 %collective-permute-start.1 = (bf16[8,64,512]{2,1,0:T(8,128)(2,1)}, bf16[8,64,512]{2,1,0:T(8,128)(2,1)S(1)}, u32[]{:S(2)}, u32[]{:S(2)}) collective-permute-start(bf16[8,64,512]{2,1,0:T(8,128)(2,1)} %relayout.1), channel_id=1, source_target_pairs={{0,2},{1,3},{2,0},{3,1},{4,6},{5,7},{6,4},{7,5},{8,10},{9,11},{10,... | collective-permute-start | bytes 1572872 | tf_op jit(solution)/shard_map/ppermute | solution.py:279
  30.9 26.3 %collective-permute-start.2 = (bf16[8,64,512]{2,1,0:T(8,128)(2,1)}, bf16[8,64,512]{2,1,0:T(8,128)(2,1)S(1)}, u32[]{:S(2)}, u32[]{:S(2)}) collective-permute-start(bf16[8,64,512]{2,1,0:T(8,128)(2,1)} %relayout.1), channel_id=1, source_target_pairs={{0,1},{1,2},{2,3},{3,0},{4,5},{5,6},{6,7},{7,4},{8,9},{9,10},{10,1... | collective-permute-start | bytes 1572872 | tf_op jit(solution)/shard_map/ppermute | solution.py:279
  63.1 1.1 copy-start
  71.0 51.5 %all-to-all-start.1 = ((bf16[128,8,256]{2,1,0:T(8,128)(2,1)}), bf16[128,8,256]{2,1,0:T(8,128)(2,1)S(1)}, u32[]{:S(2)}, u32[]{:S(2)}) async-start(bf16[128,8,256]{2,1,0:T(8,128)(2,1)} %bitcast.20), calls=%async_computation.1 | async-start | bytes 1048576 | tf_op jit(solution)/shard_map/all_to_all | solution.py:294
  86.3 16.2 %collective-permute-start.3 = (bf16[8,64,512]{2,1,0:T(8,128)(2,1)}, bf16[8,64,512]{2,1,0:T(8,128)(2,1)S(1)}, u32[]{:S(2)}, u32[]{:S(2)}) collective-permute-start(bf16[8,64,512]{2,1,0:T(8,128)(2,1)} %get-tuple-element.20), channel_id=1, source_target_pairs={{0,1},{1,2},{2,3},{3,0},{4,5},{5,6},{6,7},{7,4},{8,9},{9,10},{10,1... | collective-permute-start | bytes 1572872 | tf_op jit(solution)/shard_map/ppermute | solution.py:279
  88.2 24.9 %collective-permute-start.4 = (bf16[8,64,512]{2,1,0:T(8,128)(2,1)}, bf16[8,64,512]{2,1,0:T(8,128)(2,1)S(1)}, u32[]{:S(2)}, u32[]{:S(2)}) collective-permute-start(bf16[8,64,512]{2,1,0:T(8,128)(2,1)} %get-tuple-element.21), channel_id=1, source_target_pairs={{0,2},{1,3},{2,0},{3,1},{4,6},{5,7},{6,4},{7,5},{8,10},{9,11},{10,... | collective-permute-start | bytes 1572872 | tf_op jit(solution)/shard_map/ppermute | solution.py:279
  92.5 23.8 %collective-permute-start.5 = (bf16[8,64,512]{2,1,0:T(8,128)(2,1)}, bf16[8,64,512]{2,1,0:T(8,128)(2,1)S(1)}, u32[]{:S(2)}, u32[]{:S(2)}) collective-permute-start(bf16[8,64,512]{2,1,0:T(8,128)(2,1)} %get-tuple-element.22), channel_id=1, source_target_pairs={{0,3},{1,0},{2,1},{3,2},{4,7},{5,4},{6,5},{7,6},{8,11},{9,8},{10,9... | collective-permute-start | bytes 1572872 | tf_op jit(solution)/shard_map/ppermute | solution.py:279
  102.4 13.8 %copy-start.3 = (bf16[8,64,512]{2,1,0:T(8,128)(2,1)}, bf16[8,64,512]{2,1,0:T(8,128)(2,1)S(1)}, u32[]{:S(2)}) copy-start(bf16[8,64,512]{2,1,0:T(8,128)(2,1)S(1)} %collective-permute-done.3.refs_1_) | copy-start | bytes 1572868
  113.1 3.2 %copy-start.4 = (bf16[8,64,512]{2,1,0:T(8,128)(2,1)}, bf16[8,64,512]{2,1,0:T(8,128)(2,1)S(1)}, u32[]{:S(2)}) copy-start(bf16[8,64,512]{2,1,0:T(8,128)(2,1)S(1)} %collective-permute-done.4.refs_2_) | copy-start | bytes 1572868
  116.2 0.8 copy-start.5
  122.5 0.8 copy-start.1

commit v2 on v1

v2 whole, which is shorter than its diff:
```python
import functools

import jax
import jax.numpy as jnp
from jax import lax
from jax.experimental import pallas as pl
from jax.experimental.pallas import tpu as pltpu
from jax.sharding import PartitionSpec as P

IN = 256
NB = 8
SPLIT = 4
COLS = 512
CAP = 8
ROWS = 128
LANES = 128
WIDTH = COLS + IN

PENALTY = 10.0
LEARN_RATE = 0.001
BETA_ONE = 0.9
BETA_TWO = 0.999
EPSILON = 1e-08
WEIGHT_DECAY = 0.1
BIAS_ONE = 0.999973438601112
BIAS_TWO = 0.0952078528855534
HALF_INV_SPACING = 0.625

f32 = jnp.float32
bf16 = jnp.bfloat16


LIMIT = pltpu.CompilerParams(vmem_limit_bytes=28 * 1024 * 1024)


SCALARS = pl.BlockSpec(memory_space=pltpu.SMEM)


ANYWHERE = pl.BlockSpec(memory_space=pl.ANY)


TOKEN = jax.ShapeDtypeStruct((8, LANES), jnp.float32)


def vmem(n):
    return [pl.BlockSpec(memory_space=pltpu.VMEM) for _ in range(n)]


def slot_matrix(route_row, slots):
    wide = jnp.broadcast_to(route_row.astype(f32), (ROWS, ROWS))
    tall = jnp.transpose(wide)
    earlier = lax.broadcasted_iota(jnp.int32, (ROWS, ROWS), 0) < lax.broadcasted_iota(
        jnp.int32, (ROWS, ROWS), 1
    )
    rank = jnp.sum(jnp.where((wide == tall) & earlier, 1.0, 0.0), axis=0, keepdims=True)
    slot = route_row * CAP + rank.astype(jnp.int32)
    hit = lax.broadcasted_iota(jnp.int32, (slots, ROWS), 0) == slot
    return jnp.where(hit, 1.0, 0.0).astype(bf16)


def dispatch_kernel(route_ref, inputs_ref, grads_ref, send_ref, onehot_ref):
    experts = send_ref.shape[0]
    onehot = slot_matrix(route_ref[...], experts * CAP)
    onehot_ref[...] = onehot
    sent = jnp.dot(onehot, inputs_ref[...], preferred_element_type=f32).astype(bf16)
    sent = sent.reshape(experts, CAP, IN)
    for s in range(SPLIT):
        block = jnp.dot(
            onehot, grads_ref[:, s * COLS : (s + 1) * COLS], preferred_element_type=f32
        ).astype(bf16)
        send_ref[:, s, :, 0:COLS] = block.reshape(experts, CAP, COLS)
        send_ref[:, s, :, COLS:WIDTH] = sent


def dispatch(route_row, inputs, out_grad, experts):
    return pl.pallas_call(
        dispatch_kernel,
        out_shape=(
            jax.ShapeDtypeStruct((experts, SPLIT, CAP, WIDTH), bf16),
            jax.ShapeDtypeStruct((experts * CAP, ROWS), bf16),
        ),
        in_specs=vmem(3),
        out_specs=tuple(vmem(2)),
        name="dispatch",
    )(route_row, inputs, out_grad)


def prepare_kernel(coef_ref, out_ref, pen_ref, wide_ref):
    quarter = out_ref.shape[1]
    for j in range(COLS // LANES):
        at = slice(j * LANES, (j + 1) * LANES)
        wide_ref[j] = coef_ref[:, :, at].reshape(quarter * NB, LANES).astype(f32)
        for k in range(NB):
            out_ref[k, :, at] = wide_ref[j, pl.ds(k, quarter, stride=NB), :].astype(bf16)
    k = lax.broadcasted_iota(jnp.int32, (1, NB, COLS), 1)

    def row(values):
        out = jnp.full((1, NB, COLS), float(values[0]), f32)
        for index in range(1, NB):
            if values[index] != values[0]:
                out = jnp.where(k == index, float(values[index]), out)
        return out * PENALTY

    rows = (
        row((1, 5, 6, 6, 6, 6, 5, 1)),
        row((0, -2, -4, -4, -4, -4, -4, -2)),
        row((0, 0, 1, 1, 1, 1, 1, 1)),
        row((1, 1, 1, 1, 1, 1, 0, 0)),
        row((-2, -4, -4, -4, -4, -4, -2, 0)),
    )
    for i in range(0, quarter, 4):
        c = coef_ref[i : i + 4].astype(f32)
        pen = c * rows[0]
        for turn, weight in zip((1, 2, NB - 2, NB - 1), rows[1:]):
            pen = pen + pltpu.roll(c, turn, 1) * weight
        pen_ref[i : i + 4] = pen


def prepare(coef):
    quarter = coef.shape[0]
    return pl.pallas_call(
        prepare_kernel,
        out_shape=(
            jax.ShapeDtypeStruct((NB, quarter, COLS), bf16),
            jax.ShapeDtypeStruct((quarter, NB, COLS), f32),
        ),
        in_specs=vmem(1),
        out_specs=tuple(vmem(2)),
        scratch_shapes=[pltpu.VMEM((COLS // LANES, quarter * NB, LANES), f32)],
        compiler_params=LIMIT,
        name="prepare",
    )(coef)


def cells(x):
    t = x.astype(f32) * 1.25 + 5.5
    cell = jnp.floor(t)
    return cell, t - cell


def turned_pieces(cell, pieces):
    whole = cell.astype(jnp.int32)
    odd = (whole & 1) == 1
    high = (whole & 2) == 2
    s0, s1, s2, s3 = pieces
    a = (
        jnp.where(odd, s1, s0),
        jnp.where(odd, s0, s3),
        jnp.where(odd, s3, s2),
        jnp.where(odd, s2, s1),
    )
    v = [jnp.where(high, a[q - 2], a[q]) for q in range(4)]
    v[0] = jnp.where(cell < 8.0, v[0], 0.0)
    v[1] = jnp.where((cell >= 1.0) & (cell < 9.0), v[1], 0.0)
    v[2] = jnp.where((cell >= 2.0) & (cell < 10.0), v[2], 0.0)
    v[3] = jnp.where(cell >= 3.0, v[3], 0.0)
    return v


def assemble_kernel(place_ref, own_ref, first_ref, pair_ref, out_ref, done_ref):
    done_ref[...] = jnp.zeros_like(done_ref)
    out_ref[place_ref[0]] = own_ref[...]
    out_ref[place_ref[1]] = first_ref[...]
    out_ref[place_ref[2]] = pair_ref[0]
    out_ref[place_ref[3]] = pair_ref[1]


def assemble(place, own, first, pair):
    return pl.pallas_call(
        assemble_kernel,
        out_shape=(jax.ShapeDtypeStruct((4,) + own.shape, bf16), TOKEN),
        in_specs=[SCALARS] + vmem(3),
        out_specs=tuple(vmem(2)),
        compiler_params=LIMIT,
        name="assemble",
    )(place, own, first, pair)


def project_kernel(data_ref, coef_ref, after_ref, out_ref, done_ref, wide_ref, partial_ref, sems):
    done_ref[...] = jnp.zeros_like(done_ref)
    copies = []
    slots = data_ref.shape[0]
    step = wide_ref.shape[2]
    small = 32
    c = HALF_INV_SPACING
    for block in range(slots // step):
        at = slice(block * step, (block + 1) * step)
        for k in range(NB):
            weight = jnp.concatenate([coef_ref[q, k] for q in range(coef_ref.shape[0])], axis=0)
            wide_ref[block % 2, k] = lax.dot_general(
                data_ref[at, 0:COLS], weight, (((1,), (1,)), ((), ())), preferred_element_type=f32
            )
        for low in range(0, step, small):
            here = slice(low, low + small)
            rows = slice(block * step + low, block * step + low + small)
            cell, f = cells(data_ref[rows, COLS:WIDTH])
            g = 1.0 - f
            v = turned_pieces(
                cell,
                (
                    c * f * f,
                    c + f * (2.0 * c - 3.0 * c * f),
                    -c - g * (2.0 * c - 3.0 * c * g),
                    -c * g * g,
                ),
            )
            total = None
            for q in range(4):
                live = jnp.where(
                    cell < float(q + 4), wide_ref[block % 2, q, here], wide_ref[block % 2, q + 4, here]
                )
                term = v[q] * live
                total = term if total is None else total + term
            partial_ref[rows, :] = total.astype(bf16)
        copies.append(pltpu.make_async_copy(partial_ref.at[at], out_ref.at[at], sems.at[block]))
        copies[-1].start()
    for copy in copies:
        copy.wait()


def project(data, coefs, after):
    slots = data.shape[0]
    step = 256
    return pl.pallas_call(
        project_kernel,
        out_shape=(pltpu.HBM((slots, IN), bf16), TOKEN),
        in_specs=vmem(2) + [ANYWHERE],
        out_specs=(pl.BlockSpec(memory_space=pltpu.HBM), vmem(1)[0]),
        scratch_shapes=[
            pltpu.VMEM((2, NB, step, IN), f32),
            pltpu.VMEM((slots, IN), bf16),
            pltpu.SemaphoreType.DMA((slots // step,)),
        ],
        compiler_params=LIMIT,
        cost_estimate=pl.CostEstimate(flops=2200000000, bytes_accessed=8000000, transcendentals=0),
        name="project",
    )(data, coefs, after)


def fill_basis(basis_ref, x_ref, start, quarter):
    slots = x_ref.shape[1]
    c = 1.0 / 6.0
    high, wide = 16, 256
    for low in range(0, quarter, high):
        for left in range(0, slots, wide):
            rows = pl.ds(pl.multiple_of(start + low, high), high)
            cell, f = cells(x_ref[rows, left : left + wide])
            g = 1.0 - f
            v = turned_pieces(
                cell,
                (
                    c * f * f * f,
                    c + f * (0.5 + f * (0.5 - 0.5 * f)),
                    c + g * (0.5 + g * (0.5 - 0.5 * g)),
                    c * g * g * g,
                ),
            )
            for q in range(4):
                below = cell < float(q + 4)
                for k, value in (
                    (q, jnp.where(below, v[q], 0.0)),
                    (q + 4, jnp.where(below, 0.0, v[q])),
                ):
                    at = k * quarter + low
                    basis_ref[at : at + high, left : left + wide] = value.astype(bf16)


def bases_dot(basis_ref, turned_ref, data_ref, start, quarter):
    fill_basis(basis_ref, turned_ref, start, quarter)
    return jnp.dot(basis_ref[...], data_ref[:, 0:COLS], preferred_element_type=f32).reshape(
        NB, quarter, COLS
    )


def pair_kernel(place_ref, data_ref, after_ref, out_ref, turned_ref, done_ref, basis_ref):
    done_ref[...] = jnp.zeros_like(done_ref)
    same = lax.broadcasted_iota(jnp.int32, (IN, IN), 0) == lax.broadcasted_iota(
        jnp.int32, (IN, IN), 1
    )
    turned_ref[...] = lax.dot_general(
        jnp.where(same, 1.0, 0.0).astype(bf16),
        data_ref[:, COLS:WIDTH],
        (((1,), (1,)), ((), ())),
        preferred_element_type=f32,
    ).astype(bf16)
    quarter = out_ref.shape[2]
    for index, which in enumerate((1, 3)):
        out_ref[index] = bases_dot(
            basis_ref.at[index], turned_ref, data_ref, place_ref[which] * quarter, quarter
        ).astype(bf16)


def pair(place, data, after, quarter):
    slots = data.shape[0]
    return pl.pallas_call(
        pair_kernel,
        out_shape=(
            jax.ShapeDtypeStruct((2, NB, quarter, COLS), bf16),
            jax.ShapeDtypeStruct((IN, slots), bf16),
            TOKEN,
        ),
        in_specs=[SCALARS] + vmem(1) + [ANYWHERE],
        out_specs=tuple(vmem(3)),
        scratch_shapes=[pltpu.VMEM((2, NB * quarter, slots), bf16)],
        compiler_params=LIMIT,
        cost_estimate=pl.CostEstimate(flops=1100000000, bytes_accessed=4000000, transcendentals=0),
        name="pair",
    )(place, data, after)


def last_kernel(place_ref, turned_ref, data_ref, came_ref, after_ref, out_ref, done_ref, basis_ref):
    done_ref[...] = jnp.zeros_like(done_ref)
    quarter = out_ref.shape[1]
    piece = bases_dot(basis_ref, turned_ref, data_ref, place_ref[2] * quarter, quarter)
    out_ref[...] = (piece + came_ref[1].astype(f32)).astype(bf16)


def last_piece(place, turned, data, came, after, quarter):
    slots = data.shape[0]
    return pl.pallas_call(
        last_kernel,
        out_shape=(jax.ShapeDtypeStruct((NB, quarter, COLS), bf16), TOKEN),
        in_specs=[SCALARS] + vmem(3) + [ANYWHERE],
        out_specs=tuple(vmem(2)),
        scratch_shapes=[pltpu.VMEM((NB * quarter, slots), bf16)],
        compiler_params=LIMIT,
        name="last_piece",
    )(place, turned, data, came, after)


def own_kernel(
    place_ref, turned_ref, data_ref, came_ref, pen_ref, after_ref, out_ref, basis_ref, wide_ref
):
    quarter = out_ref.shape[0]
    piece = bases_dot(basis_ref, turned_ref, data_ref, place_ref[0] * quarter, quarter)
    piece = piece + came_ref[0].astype(f32)
    for j in range(COLS // LANES):
        lanes = slice(j * LANES, (j + 1) * LANES)
        for k in range(NB):
            wide_ref[j, pl.ds(k, quarter, stride=NB), :] = piece[k, :, lanes]
        out_ref[:, :, lanes] = wide_ref[j].reshape(quarter, NB, LANES) + pen_ref[:, :, lanes]


def own_piece(place, turned, data, came, pen, after):
    slots = data.shape[0]
    quarter = pen.shape[0]
    return pl.pallas_call(
        own_kernel,
        out_shape=jax.ShapeDtypeStruct(pen.shape, f32),
        in_specs=[SCALARS] + vmem(4) + [ANYWHERE],
        out_specs=vmem(1)[0],
        scratch_shapes=[
            pltpu.VMEM((NB * quarter, slots), bf16),
            pltpu.VMEM((COLS // LANES, NB * quarter, LANES), f32),
        ],
        compiler_params=LIMIT,
        name="own_piece",
    )(place, turned, data, came, pen, after)


def adam_kernel(
    last_ref, sum_ref, coef_ref, one_ref, two_ref, new_ref, one_out, two_out, done_ref, wide_ref
):
    done_ref[...] = jnp.zeros_like(done_ref)
    rows = coef_ref.shape[0]
    small = 4
    for j in range(COLS // LANES):
        lanes = slice(j * LANES, (j + 1) * LANES)
        for k in range(NB):
            wide_ref[j, pl.ds(k, rows, stride=NB), :] = last_ref[k, :, lanes].astype(f32)
    for low in range(0, rows, small):
        at = slice(low, low + small)
        grad = jnp.concatenate(
            [
                wide_ref[j, low * NB : (low + small) * NB].reshape(small, NB, LANES)
                for j in range(COLS // LANES)
            ],
            axis=2,
        )
        grad = grad + sum_ref[at]
        c = coef_ref[at].astype(f32)
        one = BETA_ONE * one_ref[at].astype(f32) + (1.0 - BETA_ONE) * grad
        two = BETA_TWO * two_ref[at].astype(f32) + (1.0 - BETA_TWO) * grad * grad
        scaled = two * (1.0 / BIAS_TWO)
        root = scaled * lax.rsqrt(scaled)
        update = one * (1.0 / BIAS_ONE) / (root + EPSILON)
        new_ref[at] = (c - LEARN_RATE * (update + WEIGHT_DECAY * c)).astype(bf16)
        one_out[at] = one.astype(bf16)
        two_out[at] = two.astype(bf16)


def adam(last, total, coef, one, two):
    quarter = coef.shape[0]
    return pl.pallas_call(
        adam_kernel,
        out_shape=tuple(jax.ShapeDtypeStruct(coef.shape, bf16) for _ in range(3)) + (TOKEN,),
        in_specs=vmem(5),
        out_specs=tuple(vmem(4)),
        scratch_shapes=[pltpu.VMEM((COLS // LANES, quarter * NB, LANES), f32)],
        compiler_params=LIMIT,
        name="adam",
    )(last, total, coef, one, two)


def combine_kernel(returned_ref, onehot_ref, after_ref, out_ref):
    experts = returned_ref.shape[0]
    total = returned_ref[:, 0].astype(f32)
    for s in range(1, SPLIT):
        total = total + returned_ref[:, s].astype(f32)
    total = total.astype(bf16).reshape(experts * CAP, IN)
    out_ref[...] = lax.dot_general(
        onehot_ref[...], total, (((0,), (0,)), ((), ())), preferred_element_type=f32
    ).astype(bf16)


def combine(returned, onehot, after):
    return pl.pallas_call(
        combine_kernel,
        out_shape=jax.ShapeDtypeStruct((ROWS, IN), bf16),
        in_specs=vmem(2) + [ANYWHERE],
        out_specs=vmem(1)[0],
        compiler_params=LIMIT,
        name="combine",
    )(returned, onehot, after)


def on_device(inputs, out_grad, route, coef, first_moment, second_moment):
    groups = lax.axis_size("expert")
    members = lax.axis_size("dp")
    experts = groups // SPLIT
    quarter = IN // members
    core = lax.axis_index("expert") % 2
    here = lax.axis_index("dp")
    place = jnp.stack([here, here ^ (1 + 2 * core), here ^ (3 - 2 * core), here ^ 2])

    def swap(value, masks):
        pairs = [
            (g * members + (m ^ masks[g % 2]), g * members + m)
            for g in range(groups)
            for m in range(members)
        ]
        return lax.ppermute(value, ("expert", "dp"), pairs)

    send, onehot = dispatch(route.reshape(1, ROWS), inputs, out_grad, experts)
    got = lax.all_to_all(
        send.reshape(groups, CAP, WIDTH), "expert", split_axis=0, concat_axis=0, tiled=True
    ).reshape(groups * CAP, WIDTH)

    own, pen = prepare(coef[0])
    first_coef = swap(own, (1, 3))
    coefs, done = assemble(place, own, first_coef, swap(jnp.stack([own, first_coef]), (3, 1)))

    sent, turned, done = pair(place, got, done, quarter)
    came = swap(sent, (1, 3))
    partial, done = project(got, coefs, done)
    returned = lax.all_to_all(
        partial.reshape(groups, CAP, IN), "expert", split_axis=0, concat_axis=0, tiled=True
    )
    sent_last, done = last_piece(place, turned, got, came, done, quarter)
    last = swap(sent_last, (3, 1))
    total = own_piece(place, turned, got, came, pen, done)
    new_coef, new_one, new_two, done = adam(
        last, total, coef[0], first_moment[0], second_moment[0]
    )
    input_grad = combine(returned.reshape(experts, SPLIT, CAP, IN), onehot, done)
    return input_grad, new_coef[None], new_one[None], new_two[None]


def solution(mesh):
    rows = P(("expert", "dp"), None)
    state = P("expert", "dp", None, None)
    return jax.shard_map(
        on_device,
        mesh=mesh,
        in_specs=(rows, rows, rows, state, state, state),
        out_specs=(rows, state, state, state),
        check_vma=False,
    )
```

time: 126 us -> 104 us (0.83)
  starting transfers between devices: 45.9 us -> 38.4 us
  Pallas kernels: 25.4 us -> 19.1 us
  local copies, waits for them, and re-layouts: 8.75 us -> 3.37 us
  waiting for transfers between devices: 44.3 us -> 41 us
    ppermute x6 -> x4, waiting for transfers between devices: 39.2 us -> 28.7 us  [swap(): return lax.ppermute(value, ('expert', 'dp'), pairs)]
    ppermute x6 -> x4, starting transfers between devices: 18.7 us -> 12.9 us  [swap(): return lax.ppermute(value, ('expert', 'dp'), pairs)]
    pallas_call x4 -> x7, Pallas kernels: 20.7 us -> 15.5 us  [the longest x1 4.21 us: project(): pl.pallas_call(project_kernel, out_shape=(pltpu.HBM((slots, IN), bf16), T...]
    dynamic_update_slice x4 -> x0, local copies, waits for them, and re-layouts: 4.49 us -> none  [on_device(): coef_all = lax.dynamic_update_slice(coef_all, piece, (0, at, 0))]
    all_to_all x1, waiting for transfers between devices: 0.01 us -> 4.31 us  [on_device(): lax.all_to_all(partial.reshape(groups, CAP, IN), 'expert', split_axis=0,...]
    all_to_all x1, waiting for transfers between devices: 5.05 us -> 7.9 us  [on_device(): lax.all_to_all(send.reshape(groups, CAP, WIDTH), 'expert', split_axis=0,...]
    all_to_all x1, starting transfers between devices: 8.82 us -> 6.95 us  [on_device(): lax.all_to_all(partial.reshape(groups, CAP, IN), 'expert', split_axis=0,...]
    broadcast_in_dim x1 -> x0, local copies, waits for them, and re-layouts: 1.52 us -> none  [on_device(): coef_all = jnp.zeros((NB, IN, COLS), bf16)]
  transfers between devices with their start and end apart: 8 -> 6, of which waited for: 7 -> 6; matrix products, arithmetic and copies ran while one was open for 5% -> 1% of each run, Pallas kernels for 11% -> 11%
where the time goes in v2:
time: 104 us
  waiting for transfers between devices  41 us (39%)
  starting transfers between devices  38.4 us (37%)
  Pallas kernels  19.1 us (18%)
  local copies, waits for them, and re-layouts  3.37 us (3%)
  other arithmetic  1.17 us (1%)
    ppermute x4, waiting for transfers between devices, swap(): return lax.ppermute(value, ('expert', 'dp'), pairs)  28.7 us
    all_to_all x1, starting transfers between devices, on_device(): lax.all_to_all(send.reshape(groups, CAP, WIDTH), 'expert', split_axis=0,...  18.6 us
    ppermute x4, starting transfers between devices, swap(): return lax.ppermute(value, ('expert', 'dp'), pairs)  12.9 us
    all_to_all x1, waiting for transfers between devices, on_device(): lax.all_to_all(send.reshape(groups, CAP, WIDTH), 'expert', split_axis=0,...  7.9 us
    all_to_all x1, starting transfers between devices, on_device(): lax.all_to_all(partial.reshape(groups, CAP, IN), 'expert', split_axis=0,...  6.95 us
    all_to_all x1, waiting for transfers between devices, on_device(): lax.all_to_all(partial.reshape(groups, CAP, IN), 'expert', split_axis=0,...  4.31 us
    pallas_call x1, Pallas kernels, project(): pl.pallas_call(project_kernel, out_shape=(pltpu.HBM((slots, IN), bf16), T...  4.21 us
    pallas_call x1, Pallas kernels, pair(): pl.pallas_call(pair_kernel, out_shape=(jax.ShapeDtypeStruct((2, NB, quart...  3.58 us
  transfers between devices with their start and end apart: 6, of which 6 were waited for; matrix products, arithmetic and copies ran while one was open for 1% of the time, Pallas kernels for 11%

profile of v2, /device:TPU:1, one launch (start us, length us, event | category | flops | bytes accessed | tf_op | source)
XLA Modules:
  0.0 103.8 jit_solution(2893114046439589539)
XLA Ops:
  0.6 2.8 %dispatch.1 = (bf16[32,4,8,768]{3,2,1,0:T(8,128)(2,1)}, bf16[256,128]{1,0:T(8,128)(2,1)}) custom-call(s32[1,128]{1,0:T(1,128)} %bitcast.30, bf16[128,256]{1,0:T(8,128)(2,1)} %inputs_ref.1, bf16[128,2048]{1,0:T(8,128)(2,1)} %grads_ref.1), custom_call_target="tpu_custom_call" | custom-call | tf_op jit(solution)/shard_map/dispatch/pallas_call | solution.py:76
  3.4 0.0 copy-start.2
  3.4 18.6 %all-to-all-start = ((bf16[128,8,768]{2,1,0:T(8,128)(2,1)}), bf16[128,8,768]{2,1,0:T(8,128)(2,1)S(1)}, u32[]{:S(2)}, u32[]{:S(2)}) async-start(bf16[128,8,768]{2,1,0:T(8,128)(2,1)} %bitcast.28), calls=%async_computation | async-start | bytes 3145728 | tf_op jit(solution)/shard_map/all_to_all | solution.py:445
  22.0 0.0 copy-done.2
  22.0 1.0 prepare.1
  23.0 0.0 copy-start.4
  23.0 1.0 copy-done.4
  24.0 4.4 %collective-permute-start = (bf16[8,64,512]{2,1,0:T(8,128)(2,1)S(1)}, bf16[8,64,512]{2,1,0:T(8,128)(2,1)S(1)}, u32[]{:S(2)}, u32[]{:S(2)}) collective-permute-start(bf16[8,64,512]{2,1,0:T(8,128)(2,1)S(1)} %get-tuple-element.22.own_ref), channel_id=1, source_target_pairs={{1,0},{0,1},{3,2},{2,3},{7,4},{6,5},{5,6},{4,7},{9,8},{8,9},{11,10... | collective-permute-start | bytes 1572872 | tf_op jit(solution)/shard_map/ppermute | solution.py:442
  28.3 7.0 %collective-permute-done.first_ref = bf16[8,64,512]{2,1,0:T(8,128)(2,1)S(1)} collective-permute-done((bf16[8,64,512]{2,1,0:T(8,128)(2,1)S(1)}, bf16[8,64,512]{2,1,0:T(8,128)(2,1)S(1)}, u32[]{:S(2)}, u32[]{:S(2)}) %collective-permute-start) | collective-permute-done | bytes 524320 | tf_op jit(solution)/shard_map/ppermute | solution.py:442
  35.4 1.1 %pad_maximum_fusion = bf16[2,8,64,512]{3,2,1,0:T(8,128)(2,1)} fusion(bf16[1,8,64,512]{3,2,1,0:T(8,128)(2,1)S(1)} %bitcast.23, bf16[1,8,64,512]{3,2,1,0:T(8,128)(2,1)S(1)} %bitcast.22), kind=kLoop, calls=%fused_computation | loop fusion | flops 524288 | bytes 2097152 | tf_op jit(solution)/shard_map/stack | solution.py:451
  36.5 1.9 %collective-permute-start.1 = (bf16[2,8,64,512]{3,2,1,0:T(8,128)(2,1)}, bf16[2,8,64,512]{3,2,1,0:T(8,128)(2,1)}, u32[]{:S(2)}, u32[]{:S(2)}) collective-permute-start(bf16[2,8,64,512]{3,2,1,0:T(8,128)(2,1)} %pad_maximum_fusion), channel_id=1, source_target_pairs={{3,0},{2,1},{1,2},{0,3},{5,4},{4,5},{7,6},{6,7},{11,8},{10,9},{9,1... | collective-permute-start | bytes 3145736 | tf_op jit(solution)/shard_map/ppermute | solution.py:442
  38.4 0.1 pad_add_fusion.place_ref
  38.5 14.1 %collective-permute-done.1.pair_ref = bf16[2,8,64,512]{3,2,1,0:T(8,128)(2,1)} collective-permute-done((bf16[2,8,64,512]{3,2,1,0:T(8,128)(2,1)}, bf16[2,8,64,512]{3,2,1,0:T(8,128)(2,1)}, u32[]{:S(2)}, u32[]{:S(2)}) %collective-permute-start.1) | collective-permute-done | bytes 1048608 | tf_op jit(solution)/shard_map/ppermute | solution.py:442
  52.6 1.4 %assemble.1 = (bf16[4,8,64,512]{3,2,1,0:T(8,128)(2,1)S(1)}, f32[8,128]{1,0:T(8,128)S(1)}) custom-call(s32[4]{0:T(128)S(1)} %pad_add_fusion.place_ref, bf16[8,64,512]{2,1,0:T(8,128)(2,1)S(1)} %get-tuple-element.22.own_ref, bf16[8,64,512]{2,1,0:T(8,128)(2,1)S(1)} %collective-permute-done.first_ref, bf16[2,8,64,512]{3,2,1,0:T(8,128)(2,1)} %collective-permute-done.1.pair_ref), custom_call_target="tpu_custom_call" | custom-call | tf_op jit(solution)/shard_map/assemble/pallas_call | solution.py:169
  54.0 0.0 copy-start.9
  54.0 1.3 %copy-done.9 = bf16[4,8,64,512]{3,2,1,0:T(8,128)(2,1)} copy-done((bf16[4,8,64,512]{3,2,1,0:T(8,128)(2,1)}, bf16[4,8,64,512]{3,2,1,0:T(8,128)(2,1)S(1)}, u32[]{:S(2)}) %copy-start.9) | copy-done | bytes 2097176
  55.3 7.9 %all-to-all-done = bf16[128,8,768]{2,1,0:T(8,128)(2,1)S(1)} async-done(((bf16[128,8,768]{2,1,0:T(8,128)(2,1)}), bf16[128,8,768]{2,1,0:T(8,128)(2,1)S(1)}, u32[]{:S(2)}, u32[]{:S(2)}) %all-to-all-start) | async-done | bytes 1572896 | tf_op jit(solution)/shard_map/all_to_all | solution.py:445
  63.2 0.0 copy-start.10
  63.2 3.6 %pair.1 = (bf16[2,8,64,512]{3,2,1,0:T(8,128)(2,1)}, bf16[256,1024]{1,0:T(8,128)(2,1)S(1)}, f32[8,128]{1,0:T(8,128)S(1)}) custom-call(s32[4]{0:T(128)S(1)} %pad_add_fusion.place_ref, bf16[1024,768]{1,0:T(8,128)(2,1)S(1)} %bitcast.17, f32[8,128]{1,0:T(8,128)S(1)} %get-tuple-element.24.after_ref), custom_call_target="tpu_custom_call" | custom-call | flops 1100000000 | bytes 4000000 | tf_op jit(solution)/shard_map/pair/pallas_call | solution.py:295
  66.8 0.0 copy-start
  66.8 4.4 %collective-permute-start.2 = (bf16[2,8,64,512]{3,2,1,0:T(8,128)(2,1)}, bf16[2,8,64,512]{3,2,1,0:T(8,128)(2,1)S(1)}, u32[]{:S(2)}, u32[]{:S(2)}) collective-permute-start(bf16[2,8,64,512]{3,2,1,0:T(8,128)(2,1)} %get-tuple-element.29), channel_id=1, source_target_pairs={{1,0},{0,1},{3,2},{2,3},{7,4},{6,5},{5,6},{4,7},{9,8},{8,9},{11,10... | collective-permute-start | bytes 3145736 | tf_op jit(solution)/shard_map/ppermute | solution.py:442
  71.2 0.0 copy-done.10
  71.2 4.2 %project.1 = (bf16[1024,256]{1,0:T(8,128)(2,1)}, f32[8,128]{1,0:T(8,128)S(1)}) custom-call(bf16[1024,768]{1,0:T(8,128)(2,1)S(1)} %bitcast.18, bf16[4,8,64,512]{3,2,1,0:T(8,128)(2,1)S(1)} %copy-done.10, f32[8,128]{1,0:T(8,128)S(1)} %get-tuple-element.25.after_ref), custom_call_target="tpu_custom_call" | custom-call | flops 2200000000 | bytes 8000000 | tf_op jit(solution)/shard_map/project/pallas_call | solution.py:224
  75.4 0.0 copy-done
  75.4 6.9 %all-to-all-start.1 = ((bf16[128,8,256]{2,1,0:T(8,128)(2,1)}), bf16[128,8,256]{2,1,0:T(8,128)(2,1)S(1)}, u32[]{:S(2)}, u32[]{:S(2)}) async-start(bf16[128,8,256]{2,1,0:T(8,128)(2,1)} %bitcast.29), calls=%async_computation.1 | async-start | bytes 1048576 | tf_op jit(solution)/shard_map/all_to_all | solution.py:456
  82.4 1.4 %collective-permute-done.2.came_ref = bf16[2,8,64,512]{3,2,1,0:T(8,128)(2,1)S(1)} collective-permute-done((bf16[2,8,64,512]{3,2,1,0:T(8,128)(2,1)}, bf16[2,8,64,512]{3,2,1,0:T(8,128)(2,1)S(1)}, u32[]{:S(2)}, u32[]{:S(2)}) %collective-permute-start.2) | collective-permute-done | bytes 1048608 | tf_op jit(solution)/shard_map/ppermute | solution.py:442
  83.8 0.0 copy-start.1
  83.8 1.0 %copy-done.1 = bf16[256,1024]{1,0:T(8,128)(2,1)S(1)} copy-done((bf16[256,1024]{1,0:T(8,128)(2,1)S(1)}, bf16[256,1024]{1,0:T(8,128)(2,1)}, u32[]{:S(2)}) %copy-start.1) | copy-done | bytes 524312
  84.8 0.0 copy-start.5
  84.8 1.5 %last_piece.1 = (bf16[8,64,512]{2,1,0:T(8,128)(2,1)S(1)}, f32[8,128]{1,0:T(8,128)S(1)}) custom-call(s32[4]{0:T(128)S(1)} %pad_add_fusion.place_ref, bf16[256,1024]{1,0:T(8,128)(2,1)S(1)} %copy-done.1, bf16[1024,768]{1,0:T(8,128)(2,1)S(1)} %bitcast.19, bf16[2,8,64,512]{3,2,1,0:T(8,128)(2,1)S(1)} %collective-permute-done.2.came_ref, ...), custom_call_target="tpu_custom_call" | custom-call | tf_op jit(solution)/shard_map/last_piece/pallas_call | solution.py:320
  86.3 2.2 %collective-permute-start.3 = (bf16[8,64,512]{2,1,0:T(8,128)(2,1)S(1)}, bf16[8,64,512]{2,1,0:T(8,128)(2,1)S(1)}, u32[]{:S(2)}, u32[]{:S(2)}) collective-permute-start(bf16[8,64,512]{2,1,0:T(8,128)(2,1)S(1)} %get-tuple-element.31), channel_id=1, source_target_pairs={{3,0},{2,1},{1,2},{0,3},{5,4},{4,5},{7,6},{6,7},{11,8},{10,9},{9,1... | collective-permute-start | bytes 1572872 | tf_op jit(solution)/shard_map/ppermute | solution.py:442
  88.5 0.0 copy-done.5
  88.5 0.0 copy-start.3
  88.5 0.0 copy-start.6
  88.5 0.0 copy-start.7
  88.5 1.7 %own_piece.1.sum_ref = f32[64,8,512]{2,1,0:T(8,128)S(1)} custom-call(s32[4]{0:T(128)S(1)} %pad_add_fusion.place_ref, bf16[256,1024]{1,0:T(8,128)(2,1)S(1)} %copy-done.1, bf16[1024,768]{1,0:T(8,128)(2,1)S(1)} %bitcast.20, bf16[2,8,64,512]{3,2,1,0:T(8,128)(2,1)S(1)} %collective-permute-done.2.came_ref, f32[64,8,512]{2,1,0:T(8,128)S(1)} %copy-done.5, ...), custom_call_target="tpu_custom_call" | custom-call | tf_op jit(solution)/shard_map/own_piece/pallas_call | solution.py:347
  90.3 6.2 %collective-permute-done.3.last_ref = bf16[8,64,512]{2,1,0:T(8,128)(2,1)S(1)} collective-permute-done((bf16[8,64,512]{2,1,0:T(8,128)(2,1)S(1)}, bf16[8,64,512]{2,1,0:T(8,128)(2,1)S(1)}, u32[]{:S(2)}, u32[]{:S(2)}) %collective-permute-start.3) | collective-permute-done | bytes 524320 | tf_op jit(solution)/shard_map/ppermute | solution.py:442
  96.5 0.0 copy-done.3
  96.5 0.0 copy-done.6
  96.5 0.0 copy-done.7
  96.5 0.0 copy-start.8
  96.5 2.1 %adam.1 = (bf16[64,8,512]{2,1,0:T(8,128)(2,1)}, bf16[64,8,512]{2,1,0:T(8,128)(2,1)}, bf16[64,8,512]{2,1,0:T(8,128)(2,1)}, f32[8,128]{1,0:T(8,128)S(1)}) custom-call(bf16[8,64,512]{2,1,0:T(8,128)(2,1)S(1)} %collective-permute-done.3.last_ref, f32[64,8,512]{2,1,0:T(8,128)S(1)} %own_piece.1.sum_ref, bf16[64,8,512]{2,1,0:T(8,128)(2,1)S(1)} %bitcast.25, ...), custom_call_target="tpu_custom_call" | custom-call | tf_op jit(solution)/shard_map/adam/pallas_call | solution.py:394
  98.7 4.3 %all-to-all-done.1 = bf16[128,8,256]{2,1,0:T(8,128)(2,1)S(1)} async-done(((bf16[128,8,256]{2,1,0:T(8,128)(2,1)}), bf16[128,8,256]{2,1,0:T(8,128)(2,1)S(1)}, u32[]{:S(2)}, u32[]{:S(2)}) %all-to-all-start.1) | async-done | bytes 524320 | tf_op jit(solution)/shard_map/all_to_all | solution.py:456
  103.0 0.0 copy-done.8
  103.0 0.8 combine.1
Async XLA Ops:
  3.4 18.6 %copy-start.2 = (bf16[1,64,8,512]{3,2,1,0:T(8,128)(2,1)S(1)}, bf16[1,64,8,512]{3,2,1,0:T(8,128)(2,1)}, u32[]{:S(2)}) copy-start(bf16[1,64,8,512]{3,2,1,0:T(8,128)(2,1)} %param.9) | copy-start | bytes 1572868
  3.4 59.8 %all-to-all-start = ((bf16[128,8,768]{2,1,0:T(8,128)(2,1)}), bf16[128,8,768]{2,1,0:T(8,128)(2,1)S(1)}, u32[]{:S(2)}, u32[]{:S(2)}) async-start(bf16[128,8,768]{2,1,0:T(8,128)(2,1)} %bitcast.28), calls=%async_computation | async-start | bytes 3145728 | tf_op jit(solution)/shard_map/all_to_all | solution.py:445
  23.0 1.0 copy-start.4
  24.0 11.4 %collective-permute-start = (bf16[8,64,512]{2,1,0:T(8,128)(2,1)S(1)}, bf16[8,64,512]{2,1,0:T(8,128)(2,1)S(1)}, u32[]{:S(2)}, u32[]{:S(2)}) collective-permute-start(bf16[8,64,512]{2,1,0:T(8,128)(2,1)S(1)} %get-tuple-element.22.own_ref), channel_id=1, source_target_pairs={{1,0},{0,1},{3,2},{2,3},{7,4},{6,5},{5,6},{4,7},{9,8},{8,9},{11,10... | collective-permute-start | bytes 1572872 | tf_op jit(solution)/shard_map/ppermute | solution.py:442
  36.5 16.1 %collective-permute-start.1 = (bf16[2,8,64,512]{3,2,1,0:T(8,128)(2,1)}, bf16[2,8,64,512]{3,2,1,0:T(8,128)(2,1)}, u32[]{:S(2)}, u32[]{:S(2)}) collective-permute-start(bf16[2,8,64,512]{3,2,1,0:T(8,128)(2,1)} %pad_maximum_fusion), channel_id=1, source_target_pairs={{3,0},{2,1},{1,2},{0,3},{5,4},{4,5},{7,6},{6,7},{11,8},{10,9},{9,1... | collective-permute-start | bytes 3145736 | tf_op jit(solution)/shard_map/ppermute | solution.py:442
  54.0 1.3 %copy-start.9 = (bf16[4,8,64,512]{3,2,1,0:T(8,128)(2,1)}, bf16[4,8,64,512]{3,2,1,0:T(8,128)(2,1)S(1)}, u32[]{:S(2)}) copy-start(bf16[4,8,64,512]{3,2,1,0:T(8,128)(2,1)S(1)} %get-tuple-element.23.coef_ref) | copy-start | bytes 6291460
  63.2 8.0 %copy-start.10 = (bf16[4,8,64,512]{3,2,1,0:T(8,128)(2,1)S(1)}, bf16[4,8,64,512]{3,2,1,0:T(8,128)(2,1)}, u32[]{:S(2)}) copy-start(bf16[4,8,64,512]{3,2,1,0:T(8,128)(2,1)} %copy-done.9) | copy-start | bytes 6291460
  66.8 8.6 %copy-start = (bf16[256,1024]{1,0:T(8,128)(2,1)}, bf16[256,1024]{1,0:T(8,128)(2,1)S(1)}, u32[]{:S(2)}) copy-start(bf16[256,1024]{1,0:T(8,128)(2,1)S(1)} %get-tuple-element.28.turned_ref) | copy-start | bytes 1572868
  66.8 17.0 %collective-permute-start.2 = (bf16[2,8,64,512]{3,2,1,0:T(8,128)(2,1)}, bf16[2,8,64,512]{3,2,1,0:T(8,128)(2,1)S(1)}, u32[]{:S(2)}, u32[]{:S(2)}) collective-permute-start(bf16[2,8,64,512]{3,2,1,0:T(8,128)(2,1)} %get-tuple-element.29), channel_id=1, source_target_pairs={{1,0},{0,1},{3,2},{2,3},{7,4},{6,5},{5,6},{4,7},{9,8},{8,9},{11,10... | collective-permute-start | bytes 3145736 | tf_op jit(solution)/shard_map/ppermute | solution.py:442
  75.4 27.5 %all-to-all-start.1 = ((bf16[128,8,256]{2,1,0:T(8,128)(2,1)}), bf16[128,8,256]{2,1,0:T(8,128)(2,1)S(1)}, u32[]{:S(2)}, u32[]{:S(2)}) async-start(bf16[128,8,256]{2,1,0:T(8,128)(2,1)} %bitcast.29), calls=%async_computation.1 | async-start | bytes 1048576 | tf_op jit(solution)/shard_map/all_to_all | solution.py:456
  83.8 1.0 %copy-start.1 = (bf16[256,1024]{1,0:T(8,128)(2,1)S(1)}, bf16[256,1024]{1,0:T(8,128)(2,1)}, u32[]{:S(2)}) copy-start(bf16[256,1024]{1,0:T(8,128)(2,1)} %copy-done) | copy-start | bytes 1572868
  84.8 3.7 %copy-start.5 = (f32[64,8,512]{2,1,0:T(8,128)S(1)}, f32[64,8,512]{2,1,0:T(8,128)}, u32[]{:S(2)}) copy-start(f32[64,8,512]{2,1,0:T(8,128)} %copy-done.4) | copy-start | bytes 3145732
  86.3 10.2 %collective-permute-start.3 = (bf16[8,64,512]{2,1,0:T(8,128)(2,1)S(1)}, bf16[8,64,512]{2,1,0:T(8,128)(2,1)S(1)}, u32[]{:S(2)}, u32[]{:S(2)}) collective-permute-start(bf16[8,64,512]{2,1,0:T(8,128)(2,1)S(1)} %get-tuple-element.31), channel_id=1, source_target_pairs={{3,0},{2,1},{1,2},{0,3},{5,4},{4,5},{7,6},{6,7},{11,8},{10,9},{9,1... | collective-permute-start | bytes 1572872 | tf_op jit(solution)/shard_map/ppermute | solution.py:442
  88.5 8.0 %copy-start.3 = (bf16[1,64,8,512]{3,2,1,0:T(8,128)(2,1)S(1)}, bf16[1,64,8,512]{3,2,1,0:T(8,128)(2,1)}, u32[]{:S(2)}) copy-start(bf16[1,64,8,512]{3,2,1,0:T(8,128)(2,1)} %param.9) | copy-start | bytes 1572868
  88.5 8.0 %copy-start.6 = (bf16[1,64,8,512]{3,2,1,0:T(8,128)(2,1)S(1)}, bf16[1,64,8,512]{3,2,1,0:T(8,128)(2,1)}, u32[]{:S(2)}) copy-start(bf16[1,64,8,512]{3,2,1,0:T(8,128)(2,1)} %param.10) | copy-start | bytes 1572868
  88.5 8.0 %copy-start.7 = (bf16[1,64,8,512]{3,2,1,0:T(8,128)(2,1)S(1)}, bf16[1,64,8,512]{3,2,1,0:T(8,128)(2,1)}, u32[]{:S(2)}) copy-start(bf16[1,64,8,512]{3,2,1,0:T(8,128)(2,1)} %param.11) | copy-start | bytes 1572868
  96.5 6.5 %copy-start.8 = (bf16[256,128]{1,0:T(8,128)(2,1)S(1)}, bf16[256,128]{1,0:T(8,128)(2,1)}, u32[]{:S(2)}) copy-start(bf16[256,128]{1,0:T(8,128)(2,1)} %get-tuple-element.27.onehot_ref) | copy-start | bytes 196612

commit v3 on v2

--- a/solution.py
+++ b/solution.py
@@ -14,7 +14,8 @@
 CAP = 8
 ROWS = 128
 LANES = 128
-WIDTH = COLS + IN
+HALF = IN // 2
+WIDTH = COLS + HALF
 
 PENALTY = 10.0
 LEARN_RATE = 0.001
@@ -69,7 +70,7 @@
             onehot, grads_ref[:, s * COLS : (s + 1) * COLS], preferred_element_type=f32
         ).astype(bf16)
         send_ref[:, s, :, 0:COLS] = block.reshape(experts, CAP, COLS)
-        send_ref[:, s, :, COLS:WIDTH] = sent
+        send_ref[:, s, :, COLS:WIDTH] = sent[:, :, (s % 2) * HALF : (s % 2 + 1) * HALF]
 
 
 def dispatch(route_row, inputs, out_grad, experts):
@@ -85,13 +86,29 @@
     )(route_row, inputs, out_grad)
 
 
-def prepare_kernel(coef_ref, out_ref, pen_ref, wide_ref):
+def prepare_kernel(coef_ref, out_ref, wide_ref):
     quarter = out_ref.shape[1]
     for j in range(COLS // LANES):
         at = slice(j * LANES, (j + 1) * LANES)
         wide_ref[j] = coef_ref[:, :, at].reshape(quarter * NB, LANES).astype(f32)
         for k in range(NB):
             out_ref[k, :, at] = wide_ref[j, pl.ds(k, quarter, stride=NB), :].astype(bf16)
+
+
+def prepare(coef):
+    quarter = coef.shape[0]
+    return pl.pallas_call(
+        prepare_kernel,
+        out_shape=jax.ShapeDtypeStruct((NB, quarter, COLS), bf16),
+        in_specs=vmem(1),
+        out_specs=vmem(1)[0],
+        scratch_shapes=[pltpu.VMEM((COLS // LANES, quarter * NB, LANES), f32)],
+        compiler_params=LIMIT,
+        name="prepare",
+    )(coef)
+
+
+def penalty_rows():
     k = lax.broadcasted_iota(jnp.int32, (1, NB, COLS), 1)
 
     def row(values):
@@ -101,35 +118,13 @@
                 out = jnp.where(k == index, float(values[index]), out)
         return out * PENALTY
 
-    rows = (
+    return (
         row((1, 5, 6, 6, 6, 6, 5, 1)),
         row((0, -2, -4, -4, -4, -4, -4, -2)),
         row((0, 0, 1, 1, 1, 1, 1, 1)),
         row((1, 1, 1, 1, 1, 1, 0, 0)),
         row((-2, -4, -4, -4, -4, -4, -2, 0)),
     )
-    for i in range(0, quarter, 4):
-        c = coef_ref[i : i + 4].astype(f32)
-        pen = c * rows[0]
-        for turn, weight in zip((1, 2, NB - 2, NB - 1), rows[1:]):
-            pen = pen + pltpu.roll(c, turn, 1) * weight
-        pen_ref[i : i + 4] = pen
-
-
-def prepare(coef):
-    quarter = coef.shape[0]
-    return pl.pallas_call(
-        prepare_kernel,
-        out_shape=(
-            jax.ShapeDtypeStruct((NB, quarter, COLS), bf16),
-            jax.ShapeDtypeStruct((quarter, NB, COLS), f32),
-        ),
-        in_specs=vmem(1),
-        out_specs=tuple(vmem(2)),
-        scratch_shapes=[pltpu.VMEM((COLS // LANES, quarter * NB, LANES), f32)],
-        compiler_params=LIMIT,
-        name="prepare",
-    )(coef)
 
 
 def cells(x):
@@ -157,26 +152,41 @@
     return v
 
 
-def assemble_kernel(place_ref, own_ref, first_ref, pair_ref, out_ref, done_ref):
+def assemble_kernel(place_ref, own_ref, first_ref, second_ref, third_ref, out_ref, done_ref):
     done_ref[...] = jnp.zeros_like(done_ref)
     out_ref[place_ref[0]] = own_ref[...]
     out_ref[place_ref[1]] = first_ref[...]
-    out_ref[place_ref[2]] = pair_ref[0]
-    out_ref[place_ref[3]] = pair_ref[1]
-
-
-def assemble(place, own, first, pair):
+    out_ref[place_ref[2]] = second_ref[...]
+    out_ref[place_ref[3]] = third_ref[...]
+
+
+def assemble(place, own, first, second, third):
     return pl.pallas_call(
         assemble_kernel,
         out_shape=(jax.ShapeDtypeStruct((4,) + own.shape, bf16), TOKEN),
-        in_specs=[SCALARS] + vmem(3),
+        in_specs=[SCALARS] + vmem(4),
         out_specs=tuple(vmem(2)),
         compiler_params=LIMIT,
         name="assemble",
-    )(place, own, first, pair)
-
-
-def project_kernel(data_ref, coef_ref, after_ref, out_ref, done_ref, wide_ref, partial_ref, sems):
+    )(place, own, first, second, third)
+
+
+def take_kernel(data_ref, after_ref, out_ref):
+    out_ref[...] = data_ref[:, COLS:WIDTH]
+
+
+def take(data, after):
+    return pl.pallas_call(
+        take_kernel,
+        out_shape=jax.ShapeDtypeStruct((data.shape[0], HALF), bf16),
+        in_specs=vmem(1) + [ANYWHERE],
+        out_specs=vmem(1)[0],
+        compiler_params=LIMIT,
+        name="take",
+    )(data, after)
+
+
+def project_kernel(data_ref, x_ref, coef_ref, after_ref, out_ref, done_ref, wide_ref, partial_ref, sems):
     done_ref[...] = jnp.zeros_like(done_ref)
     copies = []
     slots = data_ref.shape[0]
@@ -193,7 +203,7 @@
         for low in range(0, step, small):
             here = slice(low, low + small)
             rows = slice(block * step + low, block * step + low + small)
-            cell, f = cells(data_ref[rows, COLS:WIDTH])
+            cell, f = cells(x_ref[rows, :])
             g = 1.0 - f
             v = turned_pieces(
                 cell,
@@ -218,13 +228,13 @@
         copy.wait()
 
 
-def project(data, coefs, after):
+def project(data, x, coefs, after):
     slots = data.shape[0]
     step = 256
     return pl.pallas_call(
         project_kernel,
         out_shape=(pltpu.HBM((slots, IN), bf16), TOKEN),
-        in_specs=vmem(2) + [ANYWHERE],
+        in_specs=vmem(3) + [ANYWHERE],
         out_specs=(pl.BlockSpec(memory_space=pltpu.HBM), vmem(1)[0]),
         scratch_shapes=[
             pltpu.VMEM((2, NB, step, IN), f32),
@@ -234,7 +244,7 @@
         compiler_params=LIMIT,
         cost_estimate=pl.CostEstimate(flops=2200000000, bytes_accessed=8000000, transcendentals=0),
         name="project",
-    )(data, coefs, after)
+    )(data, x, coefs, after)
 
 
 def fill_basis(basis_ref, x_ref, start, quarter):
@@ -272,82 +282,104 @@
     )
 
 
-def pair_kernel(place_ref, data_ref, after_ref, out_ref, turned_ref, done_ref, basis_ref):
+def pair_kernel(
+    place_ref, data_ref, other_ref, out_ref, last_ref, own_ref, x_ref, done_ref, turned_ref, basis_ref,
+    piece_ref, keep_ref, sems,
+):
     done_ref[...] = jnp.zeros_like(done_ref)
-    same = lax.broadcasted_iota(jnp.int32, (IN, IN), 0) == lax.broadcasted_iota(
-        jnp.int32, (IN, IN), 1
-    )
-    turned_ref[...] = lax.dot_general(
-        jnp.where(same, 1.0, 0.0).astype(bf16),
-        data_ref[:, COLS:WIDTH],
-        (((1,), (1,)), ((), ())),
-        preferred_element_type=f32,
-    ).astype(bf16)
+    core = place_ref[4]
+    for half, x in ((core, data_ref[:, COLS:WIDTH]), (1 - core, other_ref[...])):
+        rows = pl.ds(pl.multiple_of(half * HALF, HALF), HALF)
+        turned_ref[rows, :] = jnp.transpose(x.astype(f32)).astype(bf16)
+        x_ref[:, rows] = x
     quarter = out_ref.shape[2]
+    for which, ref in ((2, keep_ref), (0, own_ref)):
+        ref[...] = turned_ref[pl.ds(pl.multiple_of(place_ref[which] * quarter, quarter), quarter), :]
+    copies = [pltpu.make_async_copy(keep_ref, last_ref, sems.at[2])]
+    copies[0].start()
     for index, which in enumerate((1, 3)):
-        out_ref[index] = bases_dot(
+        piece_ref[index] = bases_dot(
             basis_ref.at[index], turned_ref, data_ref, place_ref[which] * quarter, quarter
         ).astype(bf16)
-
-
-def pair(place, data, after, quarter):
+        copies.append(pltpu.make_async_copy(piece_ref.at[index], out_ref.at[index], sems.at[index]))
+        copies[-1].start()
+    for copy in copies:
+        copy.wait()
+
+
+def pair(place, data, other, quarter):
     slots = data.shape[0]
     return pl.pallas_call(
         pair_kernel,
         out_shape=(
-            jax.ShapeDtypeStruct((2, NB, quarter, COLS), bf16),
-            jax.ShapeDtypeStruct((IN, slots), bf16),
+            pltpu.HBM((2, NB, quarter, COLS), bf16),
+            pltpu.HBM((quarter, slots), bf16),
+            jax.ShapeDtypeStruct((quarter, slots), bf16),
+            jax.ShapeDtypeStruct((slots, IN), bf16),
             TOKEN,
         ),
-        in_specs=[SCALARS] + vmem(1) + [ANYWHERE],
-        out_specs=tuple(vmem(3)),
-        scratch_shapes=[pltpu.VMEM((2, NB * quarter, slots), bf16)],
+        in_specs=[SCALARS] + vmem(2),
+        out_specs=(pl.BlockSpec(memory_space=pltpu.HBM),) * 2 + tuple(vmem(3)),
+        scratch_shapes=[
+            pltpu.VMEM((IN, slots), bf16),
+            pltpu.VMEM((2, NB * quarter, slots), bf16),
+            pltpu.VMEM((2, NB, quarter, COLS), bf16),
+            pltpu.VMEM((quarter, slots), bf16),
+            pltpu.SemaphoreType.DMA((3,)),
+        ],
         compiler_params=LIMIT,
         cost_estimate=pl.CostEstimate(flops=1100000000, bytes_accessed=4000000, transcendentals=0),
         name="pair",
-    )(place, data, after)
-
-
-def last_kernel(place_ref, turned_ref, data_ref, came_ref, after_ref, out_ref, done_ref, basis_ref):
+    )(place, data, other)
+
+
+def last_kernel(turned_ref, data_ref, came_ref, after_ref, out_ref, done_ref, basis_ref):
     done_ref[...] = jnp.zeros_like(done_ref)
     quarter = out_ref.shape[1]
-    piece = bases_dot(basis_ref, turned_ref, data_ref, place_ref[2] * quarter, quarter)
+    piece = bases_dot(basis_ref, turned_ref, data_ref, 0, quarter)
     out_ref[...] = (piece + came_ref[1].astype(f32)).astype(bf16)
 
 
-def last_piece(place, turned, data, came, after, quarter):
+def last_piece(turned, data, came, after, quarter):
     slots = data.shape[0]
     return pl.pallas_call(
         last_kernel,
         out_shape=(jax.ShapeDtypeStruct((NB, quarter, COLS), bf16), TOKEN),
-        in_specs=[SCALARS] + vmem(3) + [ANYWHERE],
+        in_specs=vmem(3) + [ANYWHERE],
         out_specs=tuple(vmem(2)),
         scratch_shapes=[pltpu.VMEM((NB * quarter, slots), bf16)],
         compiler_params=LIMIT,
         name="last_piece",
-    )(place, turned, data, came, after)
+    )(turned, data, came, after)
 
 
 def own_kernel(
-    place_ref, turned_ref, data_ref, came_ref, pen_ref, after_ref, out_ref, basis_ref, wide_ref
+    turned_ref, data_ref, came_ref, coef_ref, after_ref, out_ref, basis_ref, wide_ref
 ):
     quarter = out_ref.shape[0]
-    piece = bases_dot(basis_ref, turned_ref, data_ref, place_ref[0] * quarter, quarter)
+    piece = bases_dot(basis_ref, turned_ref, data_ref, 0, quarter)
     piece = piece + came_ref[0].astype(f32)
     for j in range(COLS // LANES):
         lanes = slice(j * LANES, (j + 1) * LANES)
         for k in range(NB):
             wide_ref[j, pl.ds(k, quarter, stride=NB), :] = piece[k, :, lanes]
-        out_ref[:, :, lanes] = wide_ref[j].reshape(quarter, NB, LANES) + pen_ref[:, :, lanes]
-
-
-def own_piece(place, turned, data, came, pen, after):
+        out_ref[:, :, lanes] = wide_ref[j].reshape(quarter, NB, LANES)
+    rows = penalty_rows()
+    for i in range(0, quarter, 4):
+        c = coef_ref[i : i + 4].astype(f32)
+        pen = c * rows[0]
+        for turn, weight in zip((1, 2, NB - 2, NB - 1), rows[1:]):
+            pen = pen + pltpu.roll(c, turn, 1) * weight
+        out_ref[i : i + 4] = out_ref[i : i + 4] + pen
+
+
+def own_piece(turned, data, came, coef, after):
     slots = data.shape[0]
-    quarter = pen.shape[0]
+    quarter = coef.shape[0]
     return pl.pallas_call(
         own_kernel,
-        out_shape=jax.ShapeDtypeStruct(pen.shape, f32),
-        in_specs=[SCALARS] + vmem(4) + [ANYWHERE],
+        out_shape=jax.ShapeDtypeStruct(coef.shape, f32),
+        in_specs=vmem(4) + [ANYWHERE],
         out_specs=vmem(1)[0],
         scratch_shapes=[
             pltpu.VMEM((NB * quarter, slots), bf16),
@@ -355,7 +387,7 @@
         ],
         compiler_params=LIMIT,
         name="own_piece",
-    )(place, turned, data, came, pen, after)
+    )(turned, data, came, coef, after)
 
 
 def adam_kernel(
@@ -431,7 +463,7 @@
     quarter = IN // members
     core = lax.axis_index("expert") % 2
     here = lax.axis_index("dp")
-    place = jnp.stack([here, here ^ (1 + 2 * core), here ^ (3 - 2 * core), here ^ 2])
+    place = jnp.stack([here, here ^ (1 + 2 * core), here ^ (3 - 2 * core), here ^ 2, core])
 
     def swap(value, masks):
         pairs = [
@@ -446,19 +478,22 @@
         send.reshape(groups, CAP, WIDTH), "expert", split_axis=0, concat_axis=0, tiled=True
     ).reshape(groups * CAP, WIDTH)
 
-    own, pen = prepare(coef[0])
+    own = prepare(coef[0])
     first_coef = swap(own, (1, 3))
-    coefs, done = assemble(place, own, first_coef, swap(jnp.stack([own, first_coef]), (3, 1)))
-
-    sent, turned, done = pair(place, got, done, quarter)
+    second_coef = swap(own, (3, 1))
+    third_coef = swap(first_coef, (3, 1))
+    coefs, done = assemble(place, own, first_coef, second_coef, third_coef)
+
+    other = lax.ppermute(take(got, done), "expert", [(g ^ 1, g) for g in range(groups)])
+    sent, last_x, own_x, x, done = pair(place, got, other, quarter)
     came = swap(sent, (1, 3))
-    partial, done = project(got, coefs, done)
+    partial, done = project(got, x, coefs, done)
     returned = lax.all_to_all(
         partial.reshape(groups, CAP, IN), "expert", split_axis=0, concat_axis=0, tiled=True
     )
-    sent_last, done = last_piece(place, turned, got, came, done, quarter)
+    sent_last, done = last_piece(last_x, got, came, done, quarter)
     last = swap(sent_last, (3, 1))
-    total = own_piece(place, turned, got, came, pen, done)
+    total = own_piece(own_x, got, came, coef[0], done)
     new_coef, new_one, new_two, done = adam(
         last, total, coef[0], first_moment[0], second_moment[0]
     )

time: 104 us -> 103 us (level)
  starting transfers between devices: 38.4 us -> 44.7 us
  waiting for transfers between devices: 41 us -> 37.7 us
  Pallas kernels: 19.1 us -> 17.3 us
  other arithmetic: 1.17 us -> 0 us
  local copies, waits for them, and re-layouts: 3.37 us -> 2.33 us
    ppermute x4 -> x5, waiting for transfers between devices: 28.7 us -> 20.3 us  [swap(): return lax.ppermute(value, ('expert', 'dp'), pairs)]
    ppermute x4 -> x5, starting transfers between devices: 12.9 us -> 15.8 us  [swap(): return lax.ppermute(value, ('expert', 'dp'), pairs)]
    ppermute x0 -> x1, starting transfers between devices: none -> 2.44 us  [on_device(): lax.ppermute(take(got, done), 'expert', [(g ^ 1, g) for g in range(groups)])]
    all_to_all x1, waiting for transfers between devices: 7.9 us -> 10.3 us  [on_device(): lax.all_to_all(send.reshape(groups, CAP, WIDTH), 'expert', split_axis=0,...]
    all_to_all x1, waiting for transfers between devices: 4.31 us -> 5.87 us  [on_device(): lax.all_to_all(partial.reshape(groups, CAP, IN), 'expert', split_axis=0,...]
    another operation x2 -> x0, other arithmetic: 1.17 us -> none  [the longest x1 1.1 us: on_device(): jnp.stack([own, first_coef])]
    ppermute x0 -> x1, waiting for transfers between devices: none -> 1.14 us  [on_device(): lax.ppermute(take(got, done), 'expert', [(g ^ 1, g) for g in range(groups)])]
    unnamed x22 -> x14, local copies, waits for them, and re-layouts: 3.37 us -> 2.25 us
  transfers between devices with their start and end apart: 6 -> 8, of which waited for: 6 -> 8; matrix products, arithmetic and copies ran while one was open for 1% -> 0% of each run, Pallas kernels for 11% -> 10%
where the time goes in v3:
time: 103 us
  starting transfers between devices  44.7 us (43%)
  waiting for transfers between devices  37.7 us (37%)
  Pallas kernels  17.3 us (17%)
  local copies, waits for them, and re-layouts  2.33 us (2%)
    ppermute x5, waiting for transfers between devices, swap(): return lax.ppermute(value, ('expert', 'dp'), pairs)  20.3 us
    all_to_all x1, starting transfers between devices, on_device(): lax.all_to_all(send.reshape(groups, CAP, WIDTH), 'expert', split_axis=0,...  18.6 us
    ppermute x5, starting transfers between devices, swap(): return lax.ppermute(value, ('expert', 'dp'), pairs)  15.8 us
    all_to_all x1, waiting for transfers between devices, on_device(): lax.all_to_all(send.reshape(groups, CAP, WIDTH), 'expert', split_axis=0,...  10.3 us
    all_to_all x1, starting transfers between devices, on_device(): lax.all_to_all(partial.reshape(groups, CAP, IN), 'expert', split_axis=0,...  7.95 us
    all_to_all x1, waiting for transfers between devices, on_device(): lax.all_to_all(partial.reshape(groups, CAP, IN), 'expert', split_axis=0,...  5.87 us
    pallas_call x1, Pallas kernels, project(): pl.pallas_call(project_kernel, out_shape=(pltpu.HBM((slots, IN), bf16), T...  4.1 us
    pallas_call x1, Pallas kernels, pair(): pl.pallas_call(pair_kernel, out_shape=(pltpu.HBM((2, NB, quarter, COLS),...  3.34 us
  transfers between devices with their start and end apart: 8, of which 8 were waited for; matrix products, arithmetic and copies ran while one was open for 0% of the time, Pallas kernels for 10%

profile of v3, /device:TPU:1, one launch (start us, length us, event | category | flops | bytes accessed | tf_op | source)
XLA Modules:
  0.0 102.9 jit_solution(13183273286234983025)
XLA Ops:
  0.6 2.7 %dispatch.1 = (bf16[32,4,8,640]{3,2,1,0:T(8,128)(2,1)}, bf16[256,128]{1,0:T(8,128)(2,1)}) custom-call(s32[1,128]{1,0:T(1,128)} %bitcast.29, bf16[128,256]{1,0:T(8,128)(2,1)} %inputs_ref.1, bf16[128,2048]{1,0:T(8,128)(2,1)} %grads_ref.1), custom_call_target="tpu_custom_call" | custom-call | tf_op jit(solution)/shard_map/dispatch/pallas_call | solution.py:77
  3.4 0.0 copy-start
  3.4 18.6 %all-to-all-start = ((bf16[128,8,640]{2,1,0:T(8,128)(2,1)}), bf16[128,8,640]{2,1,0:T(8,128)(2,1)S(1)}, u32[]{:S(2)}, u32[]{:S(2)}) async-start(bf16[128,8,640]{2,1,0:T(8,128)(2,1)} %bitcast.27), calls=%async_computation | async-start | bytes 2621440 | tf_op jit(solution)/shard_map/all_to_all | solution.py:477
  21.9 0.0 copy-done
  21.9 0.3 prepare.1.own_ref
  22.2 4.4 %collective-permute-start = (bf16[8,64,512]{2,1,0:T(8,128)(2,1)S(1)}, bf16[8,64,512]{2,1,0:T(8,128)(2,1)S(1)}, u32[]{:S(2)}, u32[]{:S(2)}) collective-permute-start(bf16[8,64,512]{2,1,0:T(8,128)(2,1)S(1)} %prepare.1.own_ref), channel_id=1, source_target_pairs={{1,0},{0,1},{3,2},{2,3},{7,4},{6,5},{5,6},{4,7},{9,8},{8,9},{11,10... | collective-permute-start | bytes 1572872 | tf_op jit(solution)/shard_map/ppermute | solution.py:474
  26.6 1.9 %collective-permute-start.1 = (bf16[8,64,512]{2,1,0:T(8,128)(2,1)S(1)}, bf16[8,64,512]{2,1,0:T(8,128)(2,1)S(1)}, u32[]{:S(2)}, u32[]{:S(2)}) collective-permute-start(bf16[8,64,512]{2,1,0:T(8,128)(2,1)S(1)} %prepare.1.own_ref), channel_id=1, source_target_pairs={{3,0},{2,1},{1,2},{0,3},{5,4},{4,5},{7,6},{6,7},{11,8},{10,9},{9,1... | collective-permute-start | bytes 1572872 | tf_op jit(solution)/shard_map/ppermute | solution.py:474
  28.5 5.9 %collective-permute-done.first_ref = bf16[8,64,512]{2,1,0:T(8,128)(2,1)S(1)} collective-permute-done((bf16[8,64,512]{2,1,0:T(8,128)(2,1)S(1)}, bf16[8,64,512]{2,1,0:T(8,128)(2,1)S(1)}, u32[]{:S(2)}, u32[]{:S(2)}) %collective-permute-start) | collective-permute-done | bytes 524320 | tf_op jit(solution)/shard_map/ppermute | solution.py:474
  34.4 2.7 %collective-permute-start.2 = (bf16[8,64,512]{2,1,0:T(8,128)(2,1)S(1)}, bf16[8,64,512]{2,1,0:T(8,128)(2,1)}, u32[]{:S(2)}, u32[]{:S(2)}) collective-permute-start(bf16[8,64,512]{2,1,0:T(8,128)(2,1)S(1)} %collective-permute-done.first_ref), channel_id=1, source_target_pairs={{3,0},{2,1},{1,2},{0,3},{5,4},{4,5},{7,6},{6,7},{11,8},{10,9},{9,1... | collective-permute-start | bytes 1572872 | tf_op jit(solution)/shard_map/ppermute | solution.py:474
  37.2 0.1 stack.23.place_ref
  37.3 2.1 %collective-permute-done.1.second_ref = bf16[8,64,512]{2,1,0:T(8,128)(2,1)S(1)} collective-permute-done((bf16[8,64,512]{2,1,0:T(8,128)(2,1)S(1)}, bf16[8,64,512]{2,1,0:T(8,128)(2,1)S(1)}, u32[]{:S(2)}, u32[]{:S(2)}) %collective-permute-start.1) | collective-permute-done | bytes 524320 | tf_op jit(solution)/shard_map/ppermute | solution.py:474
  39.4 5.7 %collective-permute-done.2.third_ref = bf16[8,64,512]{2,1,0:T(8,128)(2,1)} collective-permute-done((bf16[8,64,512]{2,1,0:T(8,128)(2,1)S(1)}, bf16[8,64,512]{2,1,0:T(8,128)(2,1)}, u32[]{:S(2)}, u32[]{:S(2)}) %collective-permute-start.2) | collective-permute-done | bytes 524320 | tf_op jit(solution)/shard_map/ppermute | solution.py:474
  45.1 1.2 %assemble.1 = (bf16[4,8,64,512]{3,2,1,0:T(8,128)(2,1)S(1)}, f32[8,128]{1,0:T(8,128)S(1)}) custom-call(s32[5]{0:T(128)S(1)} %stack.23.place_ref, bf16[8,64,512]{2,1,0:T(8,128)(2,1)S(1)} %prepare.1.own_ref, bf16[8,64,512]{2,1,0:T(8,128)(2,1)S(1)} %collective-permute-done.first_ref, bf16[8,64,512]{2,1,0:T(8,128)(2,1)S(1)} %collective-permute-done.1.second_ref, ...), custom_call_target="tpu_custom_call" | custom-call | tf_op jit(solution)/shard_map/assemble/pallas_call | solution.py:164
  46.3 0.0 copy-start.5
  46.3 1.3 %copy-done.5 = bf16[4,8,64,512]{3,2,1,0:T(8,128)(2,1)} copy-done((bf16[4,8,64,512]{3,2,1,0:T(8,128)(2,1)}, bf16[4,8,64,512]{3,2,1,0:T(8,128)(2,1)S(1)}, u32[]{:S(2)}) %copy-start.5) | copy-done | bytes 2097176
  47.7 10.3 %all-to-all-done = bf16[128,8,640]{2,1,0:T(8,128)(2,1)S(1)} async-done(((bf16[128,8,640]{2,1,0:T(8,128)(2,1)}), bf16[128,8,640]{2,1,0:T(8,128)(2,1)S(1)}, u32[]{:S(2)}, u32[]{:S(2)}) %all-to-all-start) | async-done | bytes 1310752 | tf_op jit(solution)/shard_map/all_to_all | solution.py:477
  58.0 0.0 copy-start.6
  58.1 2.4 %collective-permute-start.3 = (bf16[1024,128]{1,0:T(8,128)(2,1)S(1)}, bf16[1024,128]{1,0:T(8,128)(2,1)S(1)}, u32[]{:S(2)}, u32[]{:S(2)}) collective-permute-start(bf16[1024,128]{1,0:T(8,128)(2,1)S(1)} %take.1), channel_id=1, source_target_pairs={{4,0},{0,4},{12,8},{8,12},{20,16},{16,20},{28,24},{24,28},{36,32},... | collective-permute-start | bytes 786440 | tf_op jit(solution)/shard_map/ppermute | solution.py:487
  60.5 1.1 %collective-permute-done.3.other_ref = bf16[1024,128]{1,0:T(8,128)(2,1)S(1)} collective-permute-done((bf16[1024,128]{1,0:T(8,128)(2,1)S(1)}, bf16[1024,128]{1,0:T(8,128)(2,1)S(1)}, u32[]{:S(2)}, u32[]{:S(2)}) %collective-permute-start.3) | collective-permute-done | bytes 262176 | tf_op jit(solution)/shard_map/ppermute | solution.py:487
  61.6 3.3 %pair.1 = (bf16[2,8,64,512]{3,2,1,0:T(8,128)(2,1)}, bf16[64,1024]{1,0:T(8,128)(2,1)}, bf16[64,1024]{1,0:T(8,128)(2,1)S(1)}, bf16[1024,256]{1,0:T(8,128)(2,1)S(1)}, f32[8,128]{1,0:T(8,128)S(1)}) custom-call(s32[5]{0:T(128)S(1)} %stack.23.place_ref, bf16[1024,640]{1,0:T(8,128)(2,1)S(1)} %bitcast.17, bf16[1024,128]{1,0:T(8,128)(2,1)S(1)} %collective-permute-done.3.other_ref), custom_call_target="tpu_custom_call" | custom-call | flops 1100000000 | bytes 4000000 | tf_op jit(solution)/shard_map/pair/pallas_call | solution.py:312
  65.0 4.4 %collective-permute-start.4 = (bf16[2,8,64,512]{3,2,1,0:T(8,128)(2,1)}, bf16[2,8,64,512]{3,2,1,0:T(8,128)(2,1)S(1)}, u32[]{:S(2)}, u32[]{:S(2)}) collective-permute-start(bf16[2,8,64,512]{3,2,1,0:T(8,128)(2,1)} %get-tuple-element.29), channel_id=1, source_target_pairs={{1,0},{0,1},{3,2},{2,3},{7,4},{6,5},{5,6},{4,7},{9,8},{8,9},{11,10... | collective-permute-start | bytes 3145736 | tf_op jit(solution)/shard_map/ppermute | solution.py:474
  69.4 0.0 copy-done.6
  69.4 4.1 %project.1 = (bf16[1024,256]{1,0:T(8,128)(2,1)}, f32[8,128]{1,0:T(8,128)S(1)}) custom-call(bf16[1024,640]{1,0:T(8,128)(2,1)S(1)} %bitcast.18, bf16[1024,256]{1,0:T(8,128)(2,1)S(1)} %get-tuple-element.23.x_ref, bf16[4,8,64,512]{3,2,1,0:T(8,128)(2,1)S(1)} %copy-done.6, f32[8,128]{1,0:T(8,128)S(1)} %get-tuple-element.25.after_ref), custom_call_target="tpu_custom_call" | custom-call | flops 2200000000 | bytes 8000000 | tf_op jit(solution)/shard_map/project/pallas_call | solution.py:234
  73.5 8.0 %all-to-all-start.1 = ((bf16[128,8,256]{2,1,0:T(8,128)(2,1)}), bf16[128,8,256]{2,1,0:T(8,128)(2,1)S(1)}, u32[]{:S(2)}, u32[]{:S(2)}) async-start(bf16[128,8,256]{2,1,0:T(8,128)(2,1)} %bitcast.28), calls=%async_computation.1 | async-start | bytes 1048576 | tf_op jit(solution)/shard_map/all_to_all | solution.py:491
  81.5 0.5 collective-permute-done.4.came_ref
  82.0 0.0 copy-start.3
  82.0 0.9 copy-done.3
  82.9 0.9 last_piece.1
  83.8 2.4 %collective-permute-start.5 = (bf16[8,64,512]{2,1,0:T(8,128)(2,1)S(1)}, bf16[8,64,512]{2,1,0:T(8,128)(2,1)S(1)}, u32[]{:S(2)}, u32[]{:S(2)}) collective-permute-start(bf16[8,64,512]{2,1,0:T(8,128)(2,1)S(1)} %get-tuple-element.31), channel_id=1, source_target_pairs={{3,0},{2,1},{1,2},{0,3},{5,4},{4,5},{7,6},{6,7},{11,8},{10,9},{9,1... | collective-permute-start | bytes 1572872 | tf_op jit(solution)/shard_map/ppermute | solution.py:474
  86.2 0.0 copy-start.1
  86.2 0.0 copy-start.2
  86.2 1.7 %own_piece.1.sum_ref = f32[64,8,512]{2,1,0:T(8,128)S(1)} custom-call(bf16[64,1024]{1,0:T(8,128)(2,1)S(1)} %get-tuple-element.32.turned_ref, bf16[1024,640]{1,0:T(8,128)(2,1)S(1)} %bitcast.20, bf16[2,8,64,512]{3,2,1,0:T(8,128)(2,1)S(1)} %collective-permute-done.4.came_ref, bf16[64,8,512]{2,1,0:T(8,128)(2,1)S(1)} %bitcast.22, ...), custom_call_target="tpu_custom_call" | custom-call | tf_op jit(solution)/shard_map/own_piece/pallas_call | solution.py:379
  87.9 6.1 %collective-permute-done.5.last_ref = bf16[8,64,512]{2,1,0:T(8,128)(2,1)S(1)} collective-permute-done((bf16[8,64,512]{2,1,0:T(8,128)(2,1)S(1)}, bf16[8,64,512]{2,1,0:T(8,128)(2,1)S(1)}, u32[]{:S(2)}, u32[]{:S(2)}) %collective-permute-start.5) | collective-permute-done | bytes 524320 | tf_op jit(solution)/shard_map/ppermute | solution.py:474
  94.0 0.0 copy-done.1
  94.0 0.0 copy-done.2
  94.0 0.0 copy-start.4
  94.0 2.2 %adam.1 = (bf16[64,8,512]{2,1,0:T(8,128)(2,1)}, bf16[64,8,512]{2,1,0:T(8,128)(2,1)}, bf16[64,8,512]{2,1,0:T(8,128)(2,1)}, f32[8,128]{1,0:T(8,128)S(1)}) custom-call(bf16[8,64,512]{2,1,0:T(8,128)(2,1)S(1)} %collective-permute-done.5.last_ref, f32[64,8,512]{2,1,0:T(8,128)S(1)} %own_piece.1.sum_ref, bf16[64,8,512]{2,1,0:T(8,128)(2,1)S(1)} %bitcast.23, ...), custom_call_target="tpu_custom_call" | custom-call | tf_op jit(solution)/shard_map/adam/pallas_call | solution.py:426
  96.2 5.9 %all-to-all-done.1 = bf16[128,8,256]{2,1,0:T(8,128)(2,1)S(1)} async-done(((bf16[128,8,256]{2,1,0:T(8,128)(2,1)}), bf16[128,8,256]{2,1,0:T(8,128)(2,1)S(1)}, u32[]{:S(2)}, u32[]{:S(2)}) %all-to-all-start.1) | async-done | bytes 524320 | tf_op jit(solution)/shard_map/all_to_all | solution.py:491
  102.0 0.0 copy-done.4
  102.0 0.8 combine.1
  (1 shorter events, 0.0 us)
Async XLA Ops:
  3.4 18.6 %copy-start = (bf16[1,64,8,512]{3,2,1,0:T(8,128)(2,1)S(1)}, bf16[1,64,8,512]{3,2,1,0:T(8,128)(2,1)}, u32[]{:S(2)}) copy-start(bf16[1,64,8,512]{3,2,1,0:T(8,128)(2,1)} %param.9) | copy-start | bytes 1572868
  3.4 54.6 %all-to-all-start = ((bf16[128,8,640]{2,1,0:T(8,128)(2,1)}), bf16[128,8,640]{2,1,0:T(8,128)(2,1)S(1)}, u32[]{:S(2)}, u32[]{:S(2)}) async-start(bf16[128,8,640]{2,1,0:T(8,128)(2,1)} %bitcast.27), calls=%async_computation | async-start | bytes 2621440 | tf_op jit(solution)/shard_map/all_to_all | solution.py:477
  22.2 12.2 %collective-permute-start = (bf16[8,64,512]{2,1,0:T(8,128)(2,1)S(1)}, bf16[8,64,512]{2,1,0:T(8,128)(2,1)S(1)}, u32[]{:S(2)}, u32[]{:S(2)}) collective-permute-start(bf16[8,64,512]{2,1,0:T(8,128)(2,1)S(1)} %prepare.1.own_ref), channel_id=1, source_target_pairs={{1,0},{0,1},{3,2},{2,3},{7,4},{6,5},{5,6},{4,7},{9,8},{8,9},{11,10... | collective-permute-start | bytes 1572872 | tf_op jit(solution)/shard_map/ppermute | solution.py:474
  26.6 12.8 %collective-permute-start.1 = (bf16[8,64,512]{2,1,0:T(8,128)(2,1)S(1)}, bf16[8,64,512]{2,1,0:T(8,128)(2,1)S(1)}, u32[]{:S(2)}, u32[]{:S(2)}) collective-permute-start(bf16[8,64,512]{2,1,0:T(8,128)(2,1)S(1)} %prepare.1.own_ref), channel_id=1, source_target_pairs={{3,0},{2,1},{1,2},{0,3},{5,4},{4,5},{7,6},{6,7},{11,8},{10,9},{9,1... | collective-permute-start | bytes 1572872 | tf_op jit(solution)/shard_map/ppermute | solution.py:474
  34.4 10.7 %collective-permute-start.2 = (bf16[8,64,512]{2,1,0:T(8,128)(2,1)S(1)}, bf16[8,64,512]{2,1,0:T(8,128)(2,1)}, u32[]{:S(2)}, u32[]{:S(2)}) collective-permute-start(bf16[8,64,512]{2,1,0:T(8,128)(2,1)S(1)} %collective-permute-done.first_ref), channel_id=1, source_target_pairs={{3,0},{2,1},{1,2},{0,3},{5,4},{4,5},{7,6},{6,7},{11,8},{10,9},{9,1... | collective-permute-start | bytes 1572872 | tf_op jit(solution)/shard_map/ppermute | solution.py:474
  46.3 1.3 %copy-start.5 = (bf16[4,8,64,512]{3,2,1,0:T(8,128)(2,1)}, bf16[4,8,64,512]{3,2,1,0:T(8,128)(2,1)S(1)}, u32[]{:S(2)}) copy-start(bf16[4,8,64,512]{3,2,1,0:T(8,128)(2,1)S(1)} %get-tuple-element.24.coef_ref) | copy-start | bytes 6291460
  58.0 11.3 %copy-start.6 = (bf16[4,8,64,512]{3,2,1,0:T(8,128)(2,1)S(1)}, bf16[4,8,64,512]{3,2,1,0:T(8,128)(2,1)}, u32[]{:S(2)}) copy-start(bf16[4,8,64,512]{3,2,1,0:T(8,128)(2,1)} %copy-done.5) | copy-start | bytes 6291460
  58.1 3.6 %collective-permute-start.3 = (bf16[1024,128]{1,0:T(8,128)(2,1)S(1)}, bf16[1024,128]{1,0:T(8,128)(2,1)S(1)}, u32[]{:S(2)}, u32[]{:S(2)}) collective-permute-start(bf16[1024,128]{1,0:T(8,128)(2,1)S(1)} %take.1), channel_id=1, source_target_pairs={{4,0},{0,4},{12,8},{8,12},{20,16},{16,20},{28,24},{24,28},{36,32},... | collective-permute-start | bytes 786440 | tf_op jit(solution)/shard_map/ppermute | solution.py:487
  65.0 17.0 %collective-permute-start.4 = (bf16[2,8,64,512]{3,2,1,0:T(8,128)(2,1)}, bf16[2,8,64,512]{3,2,1,0:T(8,128)(2,1)S(1)}, u32[]{:S(2)}, u32[]{:S(2)}) collective-permute-start(bf16[2,8,64,512]{3,2,1,0:T(8,128)(2,1)} %get-tuple-element.29), channel_id=1, source_target_pairs={{1,0},{0,1},{3,2},{2,3},{7,4},{6,5},{5,6},{4,7},{9,8},{8,9},{11,10... | collective-permute-start | bytes 3145736 | tf_op jit(solution)/shard_map/ppermute | solution.py:474
  73.5 28.5 %all-to-all-start.1 = ((bf16[128,8,256]{2,1,0:T(8,128)(2,1)}), bf16[128,8,256]{2,1,0:T(8,128)(2,1)S(1)}, u32[]{:S(2)}, u32[]{:S(2)}) async-start(bf16[128,8,256]{2,1,0:T(8,128)(2,1)} %bitcast.28), calls=%async_computation.1 | async-start | bytes 1048576 | tf_op jit(solution)/shard_map/all_to_all | solution.py:491
  82.0 0.9 copy-start.3
  83.8 10.2 %collective-permute-start.5 = (bf16[8,64,512]{2,1,0:T(8,128)(2,1)S(1)}, bf16[8,64,512]{2,1,0:T(8,128)(2,1)S(1)}, u32[]{:S(2)}, u32[]{:S(2)}) collective-permute-start(bf16[8,64,512]{2,1,0:T(8,128)(2,1)S(1)} %get-tuple-element.31), channel_id=1, source_target_pairs={{3,0},{2,1},{1,2},{0,3},{5,4},{4,5},{7,6},{6,7},{11,8},{10,9},{9,1... | collective-permute-start | bytes 1572872 | tf_op jit(solution)/shard_map/ppermute | solution.py:474
  86.2 7.8 %copy-start.1 = (bf16[1,64,8,512]{3,2,1,0:T(8,128)(2,1)S(1)}, bf16[1,64,8,512]{3,2,1,0:T(8,128)(2,1)}, u32[]{:S(2)}) copy-start(bf16[1,64,8,512]{3,2,1,0:T(8,128)(2,1)} %param.10) | copy-start | bytes 1572868
  86.2 7.8 %copy-start.2 = (bf16[1,64,8,512]{3,2,1,0:T(8,128)(2,1)S(1)}, bf16[1,64,8,512]{3,2,1,0:T(8,128)(2,1)}, u32[]{:S(2)}) copy-start(bf16[1,64,8,512]{3,2,1,0:T(8,128)(2,1)} %param.11) | copy-start | bytes 1572868
  94.0 8.0 %copy-start.4 = (bf16[256,128]{1,0:T(8,128)(2,1)S(1)}, bf16[256,128]{1,0:T(8,128)(2,1)}, u32[]{:S(2)}) copy-start(bf16[256,128]{1,0:T(8,128)(2,1)} %get-tuple-element.27.onehot_ref) | copy-start | bytes 196612

commit v4 on v3

--- a/solution.py
+++ b/solution.py
@@ -282,16 +282,34 @@
     )
 
 
+def turn_kernel(data_ref, after_ref, out_ref):
+    out_ref[...] = jnp.transpose(data_ref[:, COLS:WIDTH].astype(f32)).astype(bf16)
+
+
+def turn(data, after):
+    return pl.pallas_call(
+        turn_kernel,
+        out_shape=jax.ShapeDtypeStruct((HALF, data.shape[0]), bf16),
+        in_specs=vmem(1) + [ANYWHERE],
+        out_specs=vmem(1)[0],
+        compiler_params=LIMIT,
+        name="turn",
+    )(data, after)
+
+
 def pair_kernel(
-    place_ref, data_ref, other_ref, out_ref, last_ref, own_ref, x_ref, done_ref, turned_ref, basis_ref,
+    place_ref, data_ref, other_ref, half_ref, out_ref, last_ref, own_ref, x_ref, done_ref, turned_ref, basis_ref,
     piece_ref, keep_ref, sems,
 ):
     done_ref[...] = jnp.zeros_like(done_ref)
     core = place_ref[4]
     for half, x in ((core, data_ref[:, COLS:WIDTH]), (1 - core, other_ref[...])):
         rows = pl.ds(pl.multiple_of(half * HALF, HALF), HALF)
-        turned_ref[rows, :] = jnp.transpose(x.astype(f32)).astype(bf16)
         x_ref[:, rows] = x
+        if half is core:
+            turned_ref[rows, :] = half_ref[...]
+        else:
+            turned_ref[rows, :] = jnp.transpose(x.astype(f32)).astype(bf16)
     quarter = out_ref.shape[2]
     for which, ref in ((2, keep_ref), (0, own_ref)):
         ref[...] = turned_ref[pl.ds(pl.multiple_of(place_ref[which] * quarter, quarter), quarter), :]
@@ -307,7 +325,7 @@
         copy.wait()
 
 
-def pair(place, data, other, quarter):
+def pair(place, data, other, half, quarter):
     slots = data.shape[0]
     return pl.pallas_call(
         pair_kernel,
@@ -318,7 +336,7 @@
             jax.ShapeDtypeStruct((slots, IN), bf16),
             TOKEN,
         ),
-        in_specs=[SCALARS] + vmem(2),
+        in_specs=[SCALARS] + vmem(3),
         out_specs=(pl.BlockSpec(memory_space=pltpu.HBM),) * 2 + tuple(vmem(3)),
         scratch_shapes=[
             pltpu.VMEM((IN, slots), bf16),
@@ -330,7 +348,7 @@
         compiler_params=LIMIT,
         cost_estimate=pl.CostEstimate(flops=1100000000, bytes_accessed=4000000, transcendentals=0),
         name="pair",
-    )(place, data, other)
+    )(place, data, other, half)
 
 
 def last_kernel(turned_ref, data_ref, came_ref, after_ref, out_ref, done_ref, basis_ref):
@@ -484,8 +502,9 @@
     third_coef = swap(first_coef, (3, 1))
     coefs, done = assemble(place, own, first_coef, second_coef, third_coef)
 
-    other = lax.ppermute(take(got, done), "expert", [(g ^ 1, g) for g in range(groups)])
-    sent, last_x, own_x, x, done = pair(place, got, other, quarter)
+    half = take(got, done)
+    other = lax.ppermute(half, "expert", [(g ^ 1, g) for g in range(groups)])
+    sent, last_x, own_x, x, done = pair(place, got, other, turn(got, half), quarter)
     came = swap(sent, (1, 3))
     partial, done = project(got, x, coefs, done)
     returned = lax.all_to_all(

time: 103 us -> 103 us (level)
  no operation moved by 1% of the time
where the time goes in v4:
time: 103 us
  starting transfers between devices  44.6 us (43%)
  waiting for transfers between devices  37.5 us (36%)
  Pallas kernels  17.4 us (17%)
  local copies, waits for them, and re-layouts  2.33 us (2%)
    ppermute x5, waiting for transfers between devices, swap(): return lax.ppermute(value, ('expert', 'dp'), pairs)  20.3 us
    all_to_all x1, starting transfers between devices, on_device(): lax.all_to_all(send.reshape(groups, CAP, WIDTH), 'expert', split_axis=0,...  18.6 us
    ppermute x5, starting transfers between devices, swap(): return lax.ppermute(value, ('expert', 'dp'), pairs)  15.8 us
    all_to_all x1, waiting for transfers between devices, on_device(): lax.all_to_all(send.reshape(groups, CAP, WIDTH), 'expert', split_axis=0,...  10.3 us
    all_to_all x1, starting transfers between devices, on_device(): lax.all_to_all(partial.reshape(groups, CAP, IN), 'expert', split_axis=0,...  7.96 us
    all_to_all x1, waiting for transfers between devices, on_device(): lax.all_to_all(partial.reshape(groups, CAP, IN), 'expert', split_axis=0,...  5.89 us
    pallas_call x1, Pallas kernels, project(): pl.pallas_call(project_kernel, out_shape=(pltpu.HBM((slots, IN), bf16), T...  4.1 us
    pallas_call x1, Pallas kernels, pair(): pl.pallas_call(pair_kernel, out_shape=(pltpu.HBM((2, NB, quarter, COLS),...  3.29 us
  transfers between devices with their start and end apart: 8, of which 8 were waited for; matrix products, arithmetic and copies ran while one was open for 0% of the time, Pallas kernels for 10%

profile of v4, /device:TPU:1, one launch (start us, length us, event | category | flops | bytes accessed | tf_op | source)
XLA Modules:
  0.0 102.7 jit_solution(8676419364043948082)
XLA Ops:
  0.6 2.7 %dispatch.1 = (bf16[32,4,8,640]{3,2,1,0:T(8,128)(2,1)}, bf16[256,128]{1,0:T(8,128)(2,1)}) custom-call(s32[1,128]{1,0:T(1,128)} %bitcast.30, bf16[128,256]{1,0:T(8,128)(2,1)} %inputs_ref.1, bf16[128,2048]{1,0:T(8,128)(2,1)} %grads_ref.1), custom_call_target="tpu_custom_call" | custom-call | tf_op jit(solution)/shard_map/dispatch/pallas_call | solution.py:77
  3.4 0.0 copy-start
  3.4 18.6 %all-to-all-start = ((bf16[128,8,640]{2,1,0:T(8,128)(2,1)}), bf16[128,8,640]{2,1,0:T(8,128)(2,1)S(1)}, u32[]{:S(2)}, u32[]{:S(2)}) async-start(bf16[128,8,640]{2,1,0:T(8,128)(2,1)} %bitcast.28), calls=%async_computation | async-start | bytes 2621440 | tf_op jit(solution)/shard_map/all_to_all | solution.py:495
  21.9 0.0 copy-done
  21.9 0.3 prepare.1.own_ref
  22.2 4.4 %collective-permute-start = (bf16[8,64,512]{2,1,0:T(8,128)(2,1)S(1)}, bf16[8,64,512]{2,1,0:T(8,128)(2,1)S(1)}, u32[]{:S(2)}, u32[]{:S(2)}) collective-permute-start(bf16[8,64,512]{2,1,0:T(8,128)(2,1)S(1)} %prepare.1.own_ref), channel_id=1, source_target_pairs={{1,0},{0,1},{3,2},{2,3},{7,4},{6,5},{5,6},{4,7},{9,8},{8,9},{11,10... | collective-permute-start | bytes 1572872 | tf_op jit(solution)/shard_map/ppermute | solution.py:492
  26.6 1.9 %collective-permute-start.1 = (bf16[8,64,512]{2,1,0:T(8,128)(2,1)S(1)}, bf16[8,64,512]{2,1,0:T(8,128)(2,1)S(1)}, u32[]{:S(2)}, u32[]{:S(2)}) collective-permute-start(bf16[8,64,512]{2,1,0:T(8,128)(2,1)S(1)} %prepare.1.own_ref), channel_id=1, source_target_pairs={{3,0},{2,1},{1,2},{0,3},{5,4},{4,5},{7,6},{6,7},{11,8},{10,9},{9,1... | collective-permute-start | bytes 1572872 | tf_op jit(solution)/shard_map/ppermute | solution.py:492
  28.5 5.9 %collective-permute-done.first_ref = bf16[8,64,512]{2,1,0:T(8,128)(2,1)S(1)} collective-permute-done((bf16[8,64,512]{2,1,0:T(8,128)(2,1)S(1)}, bf16[8,64,512]{2,1,0:T(8,128)(2,1)S(1)}, u32[]{:S(2)}, u32[]{:S(2)}) %collective-permute-start) | collective-permute-done | bytes 524320 | tf_op jit(solution)/shard_map/ppermute | solution.py:492
  34.4 2.7 %collective-permute-start.2 = (bf16[8,64,512]{2,1,0:T(8,128)(2,1)S(1)}, bf16[8,64,512]{2,1,0:T(8,128)(2,1)}, u32[]{:S(2)}, u32[]{:S(2)}) collective-permute-start(bf16[8,64,512]{2,1,0:T(8,128)(2,1)S(1)} %collective-permute-done.first_ref), channel_id=1, source_target_pairs={{3,0},{2,1},{1,2},{0,3},{5,4},{4,5},{7,6},{6,7},{11,8},{10,9},{9,1... | collective-permute-start | bytes 1572872 | tf_op jit(solution)/shard_map/ppermute | solution.py:492
  37.2 0.1 stack.23.place_ref
  37.3 2.1 %collective-permute-done.1.second_ref = bf16[8,64,512]{2,1,0:T(8,128)(2,1)S(1)} collective-permute-done((bf16[8,64,512]{2,1,0:T(8,128)(2,1)S(1)}, bf16[8,64,512]{2,1,0:T(8,128)(2,1)S(1)}, u32[]{:S(2)}, u32[]{:S(2)}) %collective-permute-start.1) | collective-permute-done | bytes 524320 | tf_op jit(solution)/shard_map/ppermute | solution.py:492
  39.4 5.7 %collective-permute-done.2.third_ref = bf16[8,64,512]{2,1,0:T(8,128)(2,1)} collective-permute-done((bf16[8,64,512]{2,1,0:T(8,128)(2,1)S(1)}, bf16[8,64,512]{2,1,0:T(8,128)(2,1)}, u32[]{:S(2)}, u32[]{:S(2)}) %collective-permute-start.2) | collective-permute-done | bytes 524320 | tf_op jit(solution)/shard_map/ppermute | solution.py:492
  45.1 1.2 %assemble.1 = (bf16[4,8,64,512]{3,2,1,0:T(8,128)(2,1)S(1)}, f32[8,128]{1,0:T(8,128)S(1)}) custom-call(s32[5]{0:T(128)S(1)} %stack.23.place_ref, bf16[8,64,512]{2,1,0:T(8,128)(2,1)S(1)} %prepare.1.own_ref, bf16[8,64,512]{2,1,0:T(8,128)(2,1)S(1)} %collective-permute-done.first_ref, bf16[8,64,512]{2,1,0:T(8,128)(2,1)S(1)} %collective-permute-done.1.second_ref, ...), custom_call_target="tpu_custom_call" | custom-call | tf_op jit(solution)/shard_map/assemble/pallas_call | solution.py:164
  46.3 0.0 copy-start.5
  46.3 1.3 %copy-done.5 = bf16[4,8,64,512]{3,2,1,0:T(8,128)(2,1)} copy-done((bf16[4,8,64,512]{3,2,1,0:T(8,128)(2,1)}, bf16[4,8,64,512]{3,2,1,0:T(8,128)(2,1)S(1)}, u32[]{:S(2)}) %copy-start.5) | copy-done | bytes 2097176
  47.7 10.3 %all-to-all-done = bf16[128,8,640]{2,1,0:T(8,128)(2,1)S(1)} async-done(((bf16[128,8,640]{2,1,0:T(8,128)(2,1)}), bf16[128,8,640]{2,1,0:T(8,128)(2,1)S(1)}, u32[]{:S(2)}, u32[]{:S(2)}) %all-to-all-start) | async-done | bytes 1310752 | tf_op jit(solution)/shard_map/all_to_all | solution.py:495
  58.0 2.3 %collective-permute-start.3 = (bf16[1024,128]{1,0:T(8,128)(2,1)S(1)}, bf16[1024,128]{1,0:T(8,128)(2,1)S(1)}, u32[]{:S(2)}, u32[]{:S(2)}) collective-permute-start(bf16[1024,128]{1,0:T(8,128)(2,1)S(1)} %take.1.after_ref), channel_id=1, source_target_pairs={{4,0},{0,4},{12,8},{8,12},{20,16},{16,20},{28,24},{24,28},{36,32},... | collective-permute-start | bytes 786440 | tf_op jit(solution)/shard_map/ppermute | solution.py:506
  60.4 0.1 turn.1.half_ref
  60.5 0.0 copy-start.6
  60.5 1.0 collective-permute-done.3.other_ref
  61.5 3.3 %pair.1 = (bf16[2,8,64,512]{3,2,1,0:T(8,128)(2,1)}, bf16[64,1024]{1,0:T(8,128)(2,1)}, bf16[64,1024]{1,0:T(8,128)(2,1)S(1)}, bf16[1024,256]{1,0:T(8,128)(2,1)S(1)}, f32[8,128]{1,0:T(8,128)S(1)}) custom-call(s32[5]{0:T(128)S(1)} %stack.23.place_ref, bf16[1024,640]{1,0:T(8,128)(2,1)S(1)} %bitcast.18, bf16[1024,128]{1,0:T(8,128)(2,1)S(1)} %collective-permute-done.3.other_ref, ...), custom_call_target="tpu_custom_call" | custom-call | flops 1100000000 | bytes 4000000 | tf_op jit(solution)/shard_map/pair/pallas_call | solution.py:330
  64.8 4.4 %collective-permute-start.4 = (bf16[2,8,64,512]{3,2,1,0:T(8,128)(2,1)}, bf16[2,8,64,512]{3,2,1,0:T(8,128)(2,1)S(1)}, u32[]{:S(2)}, u32[]{:S(2)}) collective-permute-start(bf16[2,8,64,512]{3,2,1,0:T(8,128)(2,1)} %get-tuple-element.29), channel_id=1, source_target_pairs={{1,0},{0,1},{3,2},{2,3},{7,4},{6,5},{5,6},{4,7},{9,8},{8,9},{11,10... | collective-permute-start | bytes 3145736 | tf_op jit(solution)/shard_map/ppermute | solution.py:492
  69.2 0.0 copy-done.6
  69.2 4.1 %project.1 = (bf16[1024,256]{1,0:T(8,128)(2,1)}, f32[8,128]{1,0:T(8,128)S(1)}) custom-call(bf16[1024,640]{1,0:T(8,128)(2,1)S(1)} %bitcast.19, bf16[1024,256]{1,0:T(8,128)(2,1)S(1)} %get-tuple-element.23.x_ref, bf16[4,8,64,512]{3,2,1,0:T(8,128)(2,1)S(1)} %copy-done.6, f32[8,128]{1,0:T(8,128)S(1)} %get-tuple-element.25.after_ref), custom_call_target="tpu_custom_call" | custom-call | flops 2200000000 | bytes 8000000 | tf_op jit(solution)/shard_map/project/pallas_call | solution.py:234
  73.3 8.0 %all-to-all-start.1 = ((bf16[128,8,256]{2,1,0:T(8,128)(2,1)}), bf16[128,8,256]{2,1,0:T(8,128)(2,1)S(1)}, u32[]{:S(2)}, u32[]{:S(2)}) async-start(bf16[128,8,256]{2,1,0:T(8,128)(2,1)} %bitcast.29), calls=%async_computation.1 | async-start | bytes 1048576 | tf_op jit(solution)/shard_map/all_to_all | solution.py:510
  81.3 0.5 collective-permute-done.4.came_ref
  81.8 0.0 copy-start.3
  81.8 0.9 copy-done.3
  82.7 0.9 last_piece.1
  83.6 2.4 %collective-permute-start.5 = (bf16[8,64,512]{2,1,0:T(8,128)(2,1)S(1)}, bf16[8,64,512]{2,1,0:T(8,128)(2,1)S(1)}, u32[]{:S(2)}, u32[]{:S(2)}) collective-permute-start(bf16[8,64,512]{2,1,0:T(8,128)(2,1)S(1)} %get-tuple-element.31), channel_id=1, source_target_pairs={{3,0},{2,1},{1,2},{0,3},{5,4},{4,5},{7,6},{6,7},{11,8},{10,9},{9,1... | collective-permute-start | bytes 1572872 | tf_op jit(solution)/shard_map/ppermute | solution.py:492
  86.0 0.0 copy-start.1
  86.0 0.0 copy-start.2
  86.0 1.7 %own_piece.1.sum_ref = f32[64,8,512]{2,1,0:T(8,128)S(1)} custom-call(bf16[64,1024]{1,0:T(8,128)(2,1)S(1)} %get-tuple-element.32.turned_ref, bf16[1024,640]{1,0:T(8,128)(2,1)S(1)} %bitcast.21, bf16[2,8,64,512]{3,2,1,0:T(8,128)(2,1)S(1)} %collective-permute-done.4.came_ref, bf16[64,8,512]{2,1,0:T(8,128)(2,1)S(1)} %bitcast.23, ...), custom_call_target="tpu_custom_call" | custom-call | tf_op jit(solution)/shard_map/own_piece/pallas_call | solution.py:397
  87.7 6.1 %collective-permute-done.5.last_ref = bf16[8,64,512]{2,1,0:T(8,128)(2,1)S(1)} collective-permute-done((bf16[8,64,512]{2,1,0:T(8,128)(2,1)S(1)}, bf16[8,64,512]{2,1,0:T(8,128)(2,1)S(1)}, u32[]{:S(2)}, u32[]{:S(2)}) %collective-permute-start.5) | collective-permute-done | bytes 524320 | tf_op jit(solution)/shard_map/ppermute | solution.py:492
  93.8 0.0 copy-done.1
  93.8 0.0 copy-done.2
  93.8 0.0 copy-start.4
  93.8 2.2 %adam.1 = (bf16[64,8,512]{2,1,0:T(8,128)(2,1)}, bf16[64,8,512]{2,1,0:T(8,128)(2,1)}, bf16[64,8,512]{2,1,0:T(8,128)(2,1)}, f32[8,128]{1,0:T(8,128)S(1)}) custom-call(bf16[8,64,512]{2,1,0:T(8,128)(2,1)S(1)} %collective-permute-done.5.last_ref, f32[64,8,512]{2,1,0:T(8,128)S(1)} %own_piece.1.sum_ref, bf16[64,8,512]{2,1,0:T(8,128)(2,1)S(1)} %bitcast.24, ...), custom_call_target="tpu_custom_call" | custom-call | tf_op jit(solution)/shard_map/adam/pallas_call | solution.py:444
  96.0 5.9 %all-to-all-done.1 = bf16[128,8,256]{2,1,0:T(8,128)(2,1)S(1)} async-done(((bf16[128,8,256]{2,1,0:T(8,128)(2,1)}), bf16[128,8,256]{2,1,0:T(8,128)(2,1)S(1)}, u32[]{:S(2)}, u32[]{:S(2)}) %all-to-all-start.1) | async-done | bytes 524320 | tf_op jit(solution)/shard_map/all_to_all | solution.py:510
  101.9 0.0 copy-done.4
  101.9 0.8 combine.1
  (1 shorter events, 0.0 us)
Async XLA Ops:
  3.4 18.6 %copy-start = (bf16[1,64,8,512]{3,2,1,0:T(8,128)(2,1)S(1)}, bf16[1,64,8,512]{3,2,1,0:T(8,128)(2,1)}, u32[]{:S(2)}) copy-start(bf16[1,64,8,512]{3,2,1,0:T(8,128)(2,1)} %param.9) | copy-start | bytes 1572868
  3.4 54.6 %all-to-all-start = ((bf16[128,8,640]{2,1,0:T(8,128)(2,1)}), bf16[128,8,640]{2,1,0:T(8,128)(2,1)S(1)}, u32[]{:S(2)}, u32[]{:S(2)}) async-start(bf16[128,8,640]{2,1,0:T(8,128)(2,1)} %bitcast.28), calls=%async_computation | async-start | bytes 2621440 | tf_op jit(solution)/shard_map/all_to_all | solution.py:495
  22.2 12.2 %collective-permute-start = (bf16[8,64,512]{2,1,0:T(8,128)(2,1)S(1)}, bf16[8,64,512]{2,1,0:T(8,128)(2,1)S(1)}, u32[]{:S(2)}, u32[]{:S(2)}) collective-permute-start(bf16[8,64,512]{2,1,0:T(8,128)(2,1)S(1)} %prepare.1.own_ref), channel_id=1, source_target_pairs={{1,0},{0,1},{3,2},{2,3},{7,4},{6,5},{5,6},{4,7},{9,8},{8,9},{11,10... | collective-permute-start | bytes 1572872 | tf_op jit(solution)/shard_map/ppermute | solution.py:492
  26.6 12.8 %collective-permute-start.1 = (bf16[8,64,512]{2,1,0:T(8,128)(2,1)S(1)}, bf16[8,64,512]{2,1,0:T(8,128)(2,1)S(1)}, u32[]{:S(2)}, u32[]{:S(2)}) collective-permute-start(bf16[8,64,512]{2,1,0:T(8,128)(2,1)S(1)} %prepare.1.own_ref), channel_id=1, source_target_pairs={{3,0},{2,1},{1,2},{0,3},{5,4},{4,5},{7,6},{6,7},{11,8},{10,9},{9,1... | collective-permute-start | bytes 1572872 | tf_op jit(solution)/shard_map/ppermute | solution.py:492
  34.4 10.7 %collective-permute-start.2 = (bf16[8,64,512]{2,1,0:T(8,128)(2,1)S(1)}, bf16[8,64,512]{2,1,0:T(8,128)(2,1)}, u32[]{:S(2)}, u32[]{:S(2)}) collective-permute-start(bf16[8,64,512]{2,1,0:T(8,128)(2,1)S(1)} %collective-permute-done.first_ref), channel_id=1, source_target_pairs={{3,0},{2,1},{1,2},{0,3},{5,4},{4,5},{7,6},{6,7},{11,8},{10,9},{9,1... | collective-permute-start | bytes 1572872 | tf_op jit(solution)/shard_map/ppermute | solution.py:492
  46.3 1.3 %copy-start.5 = (bf16[4,8,64,512]{3,2,1,0:T(8,128)(2,1)}, bf16[4,8,64,512]{3,2,1,0:T(8,128)(2,1)S(1)}, u32[]{:S(2)}) copy-start(bf16[4,8,64,512]{3,2,1,0:T(8,128)(2,1)S(1)} %get-tuple-element.24.coef_ref) | copy-start | bytes 6291460
  58.0 3.5 %collective-permute-start.3 = (bf16[1024,128]{1,0:T(8,128)(2,1)S(1)}, bf16[1024,128]{1,0:T(8,128)(2,1)S(1)}, u32[]{:S(2)}, u32[]{:S(2)}) collective-permute-start(bf16[1024,128]{1,0:T(8,128)(2,1)S(1)} %take.1.after_ref), channel_id=1, source_target_pairs={{4,0},{0,4},{12,8},{8,12},{20,16},{16,20},{28,24},{24,28},{36,32},... | collective-permute-start | bytes 786440 | tf_op jit(solution)/shard_map/ppermute | solution.py:506
  60.5 8.7 %copy-start.6 = (bf16[4,8,64,512]{3,2,1,0:T(8,128)(2,1)S(1)}, bf16[4,8,64,512]{3,2,1,0:T(8,128)(2,1)}, u32[]{:S(2)}) copy-start(bf16[4,8,64,512]{3,2,1,0:T(8,128)(2,1)} %copy-done.5) | copy-start | bytes 6291460
  64.8 17.0 %collective-permute-start.4 = (bf16[2,8,64,512]{3,2,1,0:T(8,128)(2,1)}, bf16[2,8,64,512]{3,2,1,0:T(8,128)(2,1)S(1)}, u32[]{:S(2)}, u32[]{:S(2)}) collective-permute-start(bf16[2,8,64,512]{3,2,1,0:T(8,128)(2,1)} %get-tuple-element.29), channel_id=1, source_target_pairs={{1,0},{0,1},{3,2},{2,3},{7,4},{6,5},{5,6},{4,7},{9,8},{8,9},{11,10... | collective-permute-start | bytes 3145736 | tf_op jit(solution)/shard_map/ppermute | solution.py:492
  73.3 28.5 %all-to-all-start.1 = ((bf16[128,8,256]{2,1,0:T(8,128)(2,1)}), bf16[128,8,256]{2,1,0:T(8,128)(2,1)S(1)}, u32[]{:S(2)}, u32[]{:S(2)}) async-start(bf16[128,8,256]{2,1,0:T(8,128)(2,1)} %bitcast.29), calls=%async_computation.1 | async-start | bytes 1048576 | tf_op jit(solution)/shard_map/all_to_all | solution.py:510
  81.8 0.9 copy-start.3
  83.6 10.2 %collective-permute-start.5 = (bf16[8,64,512]{2,1,0:T(8,128)(2,1)S(1)}, bf16[8,64,512]{2,1,0:T(8,128)(2,1)S(1)}, u32[]{:S(2)}, u32[]{:S(2)}) collective-permute-start(bf16[8,64,512]{2,1,0:T(8,128)(2,1)S(1)} %get-tuple-element.31), channel_id=1, source_target_pairs={{3,0},{2,1},{1,2},{0,3},{5,4},{4,5},{7,6},{6,7},{11,8},{10,9},{9,1... | collective-permute-start | bytes 1572872 | tf_op jit(solution)/shard_map/ppermute | solution.py:492
  86.0 7.8 %copy-start.1 = (bf16[1,64,8,512]{3,2,1,0:T(8,128)(2,1)S(1)}, bf16[1,64,8,512]{3,2,1,0:T(8,128)(2,1)}, u32[]{:S(2)}) copy-start(bf16[1,64,8,512]{3,2,1,0:T(8,128)(2,1)} %param.10) | copy-start | bytes 1572868
  86.0 7.8 %copy-start.2 = (bf16[1,64,8,512]{3,2,1,0:T(8,128)(2,1)S(1)}, bf16[1,64,8,512]{3,2,1,0:T(8,128)(2,1)}, u32[]{:S(2)}) copy-start(bf16[1,64,8,512]{3,2,1,0:T(8,128)(2,1)} %param.11) | copy-start | bytes 1572868
  93.8 8.0 %copy-start.4 = (bf16[256,128]{1,0:T(8,128)(2,1)S(1)}, bf16[256,128]{1,0:T(8,128)(2,1)}, u32[]{:S(2)}) copy-start(bf16[256,128]{1,0:T(8,128)(2,1)} %get-tuple-element.27.onehot_ref) | copy-start | bytes 196612
